TPU v7x, 32 devices: a whole 2x2x4 slice. The times are simulated.
32 devices in a mesh: dp: 8 (over z, y), mp: 4 (over x, core).
Axes of the slice: x: 2, y: 2, z: 4, core: 2. Of those that a mesh axis runs over, the one named last changes fastest.
Arguments:
- frames: bfloat16 [4, 4608, 768], P(None, ('dp', 'mp')), may hold values from -6 to 6
- clip_ids: int32 [4, 4608], replicated, may hold values from 0 to 5, never falling along the last dimension, each value on 1 to 1500 neighbouring positions
- w_qkv: bfloat16 [768, 3, 768], P('dp', None, 'mp'), may hold values from -0.21875 to 0.21875
- b_qv: bfloat16 [2, 4, 192], P(None, 'mp', 'dp'), may hold values from -3 to 3
- w_out: bfloat16 [768, 768], P('mp', 'dp'), may hold values from -2.5 to 2.5
- w_up: bfloat16 [768, 3072], P('dp', 'mp'), may hold values from -0.21875 to 0.21875
- b_up: bfloat16 [4, 768], P('mp', 'dp'), may hold values from -3 to 3
- w_down: bfloat16 [3072, 768], P('mp', 'dp'), may hold values from -0.109375 to 0.109375
- gains: bfloat16 [2, 768], P(None, ('dp', 'mp')), may hold values from 0.099609375 to 1.8984375
- biases: bfloat16 [4, 768], P(None, ('dp', 'mp')), may hold values from -3 to 3
- cotangent: bfloat16 [4, 4608, 768], P(None, ('dp', 'mp')), may hold values from -6 to 6
Outputs:
- output: bfloat16 [4, 4608, 768], P(None, ('dp', 'mp'))
- frames_grad: bfloat16 [4, 4608, 768], P(None, ('dp', 'mp'))
- grad_qkv: float32 [768, 3, 768], P('dp', None, 'mp')
- grad_bqv: float32 [2, 4, 192], P(None, 'mp', 'dp')
- grad_out: float32 [768, 768], P('mp', 'dp')
- grad_up: float32 [768, 3072], P('dp', 'mp')
- grad_bup: float32 [4, 768], P('mp', 'dp')
- grad_down: float32 [3072, 768], P('mp', 'dp')
- grad_gains: float32 [2, 768], P(None, ('dp', 'mp'))
- grad_biases: float32 [4, 768], P(None, ('dp', 'mp'))
Inputs may be any that keep to these rules, and one draw needn't show every extreme that they name: `clip_ids`: in each micro-batch the clip ids never fall along the frames; each clip is a run of 1 to 1500 frames, and one clip of each micro-batch has exactly 1500.
All inputs are finite; a program needn't handle non-finite values.
Results may differ from a plain program's by a relative error of at most 0.017.
Values may be sent and summed in bfloat16 or wider, within the bound.
No kernel may reach another device: no remote copies, remote signals or barrier semaphores. Data moves between devices by JAX's collectives and lax.ppermute only.
A program may use at most 192 MiB of HBM per device.

v0:
```python
import jax
import jax.numpy as jnp
from jax import lax
from jax.sharding import PartitionSpec as P

D = 768
HD = 64
CLIP = 1500
epsilon = 1e-05
masked_score = -1e30


def passed_along(array, axis, by):
    peers = lax.axis_size(axis)
    pairs = [(i, i + by) for i in range(peers) if 0 <= i + by < peers]
    return lax.ppermute(array, axis, pairs)


def shortened(array):
    return jax.tree.map(lambda a: a.astype(jnp.bfloat16) if a.dtype == jnp.float32 else a, array)


def normalize(values, gain_row, shift_row):
    middle = jnp.mean(values, axis=-1, keepdims=True)
    centred = values - middle
    spread_sq = jnp.mean(centred * centred, axis=-1, keepdims=True)
    return centred * lax.rsqrt(spread_sq + epsilon) * gain_row + shift_row


def gelu_exact(values):
    return jax.nn.gelu(values, approximate=False)


def fetch_weights(w_qkv, b_qv, w_out, w_up, b_up, w_down, gains, biases):
    gathered = (
        lax.all_gather(w_qkv, "dp", axis=0, tiled=True),
        lax.all_gather(b_qv, "dp", axis=2, tiled=True),
        lax.all_gather(w_out, "dp", axis=1, tiled=True),
        lax.all_gather(w_up, "dp", axis=0, tiled=True),
        lax.all_gather(b_up, "dp", axis=1, tiled=True),
        lax.all_gather(w_down, "dp", axis=1, tiled=True),
    )
    norm_rows = (
        lax.all_gather(gains, ("dp", "mp"), axis=1, tiled=True),
        lax.all_gather(biases, ("dp", "mp"), axis=1, tiled=True),
    )
    return (gathered, norm_rows)


def spread_rows(values):
    return lax.all_gather(values, "mp", axis=0, tiled=True)


def spread_grads(values):
    return lax.all_gather(values, "mp", axis=0, tiled=True)


def project_sum(left, weight, share_rows):

    def term(row_start, row_count):
        row_piece = lax.dynamic_slice_in_dim(left, row_start, row_count, 0)
        return jnp.dot(row_piece, weight, preferred_element_type=jnp.float32)

    return lax.psum_scatter(
        term(jnp.int32(0), share_rows * lax.axis_size("mp")).astype(jnp.bfloat16),
        "mp",
        scatter_dimension=0,
        tiled=True,
    ).astype(jnp.float32)


def project_back(left, weight, share_rows):

    def term(row_start, row_count):
        row_piece = lax.dynamic_slice_in_dim(left, row_start, row_count, 0)
        return lax.dot_general(
            row_piece, weight, (((1,), (1,)), ((), ())), preferred_element_type=jnp.float32
        )

    return lax.psum_scatter(
        term(jnp.int32(0), share_rows * lax.axis_size("mp")).astype(jnp.bfloat16),
        "mp",
        scatter_dimension=0,
        tiled=True,
    ).astype(jnp.float32)


def head_scores(query_head, key_head, same_clip):
    scores = jnp.einsum(
        "qd,kd->qk", query_head, key_head, preferred_element_type=jnp.float32
    ) * HD ** (-0.5)
    return jnp.where(same_clip, scores, masked_score)


def local(frames, clip_ids, w_qkv, b_qv, w_out, w_up, b_up, w_down, gains, biases, cotangent):
    share_rows = frames.shape[1]
    row_total = share_rows * lax.axis_size("mp")
    device = lax.axis_index("dp")
    frame_total = clip_ids.shape[1]
    width_local = w_qkv.shape[2]
    ff_local = w_up.shape[1]
    heads_local = width_local // HD
    reach_devs = (CLIP + row_total - 2) // row_total
    offsets = list(range(-reach_devs, reach_devs + 1))
    window = len(offsets) * row_total
    score_scale = HD ** (-0.5)
    key_place = (device - reach_devs) * row_total + jnp.arange(window, dtype=jnp.int32)
    key_valid = (key_place >= 0) & (key_place < frame_total)
    key_index = jnp.clip(key_place, 0, frame_total - 1)
    query_index = device * row_total + jnp.arange(row_total, dtype=jnp.int32)

    def forward_pass(inputs, clip_row, fetched):
        weights, norm_rows = fetched
        weight_qkv, bias_qv, weight_out, weight_up, bias_up, weight_down = weights
        gain_rows = norm_rows[0].astype(jnp.float32)
        bias_rows = norm_rows[1].astype(jnp.float32)
        key_clip = jnp.where(key_valid, jnp.take(clip_row, key_index), -1)
        query_clip = jnp.take(clip_row, query_index)
        same_clip = query_clip[:, None] == key_clip[None, :]
        resid_in = inputs.astype(jnp.float32)
        normed_one = normalize(resid_in, gain_rows[0], bias_rows[0]).astype(jnp.bfloat16)
        rows_one = spread_rows(normed_one)
        projected = jnp.dot(
            rows_one,
            weight_qkv.reshape(weight_qkv.shape[0], -1),
            preferred_element_type=jnp.float32,
        ).reshape(row_total, 3, width_local)
        bias_pair = bias_qv.reshape(2, width_local).astype(jnp.float32)
        projected = (
            projected + jnp.stack([bias_pair[0], jnp.zeros_like(bias_pair[0]), bias_pair[1]])[None]
        )
        projected = projected.astype(jnp.bfloat16)
        queries = projected[:, 0]
        key_value = projected[:, 1:]
        pieces = []
        for offset in offsets:
            if offset == 0:
                pieces.append(key_value)
            else:
                pieces.append(passed_along(key_value, "dp", -offset))
        near_rows = jnp.concatenate(pieces, axis=0)
        keys_near = near_rows[:, 0]
        values_near = near_rows[:, 1]
        head_outs = []
        log_totals = []
        for head_index in range(heads_local):
            columns = slice(head_index * HD, (head_index + 1) * HD)
            scores = head_scores(queries[:, columns], keys_near[:, columns], same_clip)
            top_score = jnp.max(scores, axis=-1, keepdims=True)
            log_total = top_score + jnp.log(
                jnp.sum(jnp.exp(scores - top_score), axis=-1, keepdims=True)
            )
            soft_weights = jnp.exp(scores - log_total).astype(jnp.bfloat16)
            head_outs.append(
                jnp.dot(soft_weights, values_near[:, columns], preferred_element_type=jnp.float32)
            )
            log_totals.append(log_total)
        attended = jnp.concatenate(head_outs, axis=-1).astype(jnp.bfloat16)
        mixed_rows = resid_in + project_sum(attended, weight_out, share_rows) + bias_rows[1]
        normed_two = normalize(mixed_rows, gain_rows[1], bias_rows[2]).astype(jnp.bfloat16)
        rows_two = spread_rows(normed_two)
        hidden = jnp.dot(rows_two, weight_up, preferred_element_type=jnp.float32) + bias_up.reshape(
            -1
        ).astype(jnp.float32)
        activated = gelu_exact(hidden).astype(jnp.bfloat16)
        result = mixed_rows + project_sum(activated, weight_down, share_rows) + bias_rows[3]
        kept_state = (
            resid_in,
            rows_one,
            queries,
            keys_near,
            values_near,
            same_clip,
            log_totals,
            attended,
            mixed_rows,
            rows_two,
            hidden,
            activated,
            query_clip,
            clip_row,
        )
        return (kept_state, result)

    def backward_pass(kept_state, cot_rows, fetched):
        weights, norm_rows = fetched
        weight_qkv, bias_qv, weight_out, weight_up, bias_up, weight_down = weights
        gain_rows = norm_rows[0].astype(jnp.float32)
        bias_rows = norm_rows[1].astype(jnp.float32)
        (
            resid_in,
            rows_one,
            queries,
            keys_near,
            values_near,
            same_clip,
            log_totals,
            attended,
            mixed_rows,
            rows_two,
            hidden,
            activated,
            query_clip,
            clip_row,
        ) = kept_state
        grad_result = cot_rows.astype(jnp.float32)
        rows_result = spread_grads(grad_result.astype(jnp.bfloat16))
        grad_wdown = jnp.einsum(
            "nf,nd->fd", activated, rows_result, preferred_element_type=jnp.float32
        )
        grad_act = lax.dot_general(
            rows_result, weight_down, (((1,), (1,)), ((), ())), preferred_element_type=jnp.float32
        )
        gelu_pull = jax.vjp(gelu_exact, hidden)[1]
        grad_hidden = gelu_pull(grad_act)[0].astype(jnp.bfloat16)
        grad_wup = jnp.einsum(
            "nd,nf->df", rows_two, grad_hidden, preferred_element_type=jnp.float32
        )
        grad_bup = jnp.sum(grad_hidden, axis=0, dtype=jnp.float32).reshape(1, ff_local)
        grad_two = project_back(grad_hidden, weight_up, share_rows)
        norm_pull_two = jax.vjp(normalize, mixed_rows, gain_rows[1], bias_rows[2])[1]
        grad_mix, grad_gain_two, grad_bias_two = norm_pull_two(grad_two)
        grad_mixed = grad_result + grad_mix
        rows_mixed = spread_grads(grad_mixed.astype(jnp.bfloat16))
        grad_wout = jnp.einsum(
            "nh,nd->hd", attended, rows_mixed, preferred_element_type=jnp.float32
        )
        grad_att = lax.dot_general(
            rows_mixed, weight_out, (((1,), (1,)), ((), ())), preferred_element_type=jnp.float32
        ).astype(jnp.bfloat16)
        query_grads = []
        key_grads = []
        value_grads = []
        row_deltas = []
        for head_index in range(heads_local):
            columns = slice(head_index * HD, (head_index + 1) * HD)
            query_head = queries[:, columns]
            key_head = keys_near[:, columns]
            grad_head = grad_att[:, columns]
            scores = head_scores(query_head, key_head, same_clip)
            soft_weights = jnp.exp(scores - log_totals[head_index])
            grad_soft = jnp.einsum(
                "qd,kd->qk", grad_head, values_near[:, columns], preferred_element_type=jnp.float32
            )
            row_delta = jnp.sum(grad_soft * soft_weights, axis=-1, keepdims=True)
            row_deltas.append(row_delta)
            grad_scores = (soft_weights * (grad_soft - row_delta)).astype(jnp.bfloat16)
            query_grads.append(
                jnp.dot(grad_scores, key_head, preferred_element_type=jnp.float32) * score_scale
            )
            key_grads.append(
                jnp.einsum("qk,qd->kd", grad_scores, query_head, preferred_element_type=jnp.float32)
                * score_scale
            )
            value_grads.append(
                jnp.einsum(
                    "qk,qd->kd",
                    soft_weights.astype(jnp.bfloat16),
                    grad_head,
                    preferred_element_type=jnp.float32,
                )
            )
        grad_queries = jnp.concatenate(query_grads, axis=-1)
        kv_total = jnp.zeros((row_total, 2, width_local), jnp.float32)
        stacked = jnp.stack(
            [jnp.concatenate(key_grads, axis=-1), jnp.concatenate(value_grads, axis=-1)], axis=1
        )
        for place_index, offset in enumerate(offsets):
            segment_grad = stacked[place_index * row_total : (place_index + 1) * row_total]
            if offset == 0:
                kv_total = kv_total + segment_grad
            else:
                kv_total = kv_total + passed_along(shortened(segment_grad), "dp", offset).astype(
                    segment_grad.dtype
                )
        grad_proj = jnp.concatenate([grad_queries[:, None], kv_total], axis=1).astype(jnp.bfloat16)
        grad_wqkv = jnp.einsum(
            "nd,nce->dce", rows_one, grad_proj, preferred_element_type=jnp.float32
        )
        grad_bqv = jnp.stack(
            [
                jnp.sum(grad_proj[:, 0], axis=0, dtype=jnp.float32),
                jnp.sum(grad_proj[:, 2], axis=0, dtype=jnp.float32),
            ]
        ).reshape(2, 1, width_local)
        grad_one = project_back(
            grad_proj.reshape(row_total, -1),
            weight_qkv.reshape(weight_qkv.shape[0], -1),
            share_rows,
        )
        norm_pull_one = jax.vjp(normalize, resid_in, gain_rows[0], bias_rows[0])[1]
        grad_in_norm, grad_gain_one, grad_bias_one = norm_pull_one(grad_one)
        grad_inputs = (grad_mixed + grad_in_norm).astype(jnp.bfloat16)
        grad_gain_rows = jnp.stack([grad_gain_one, grad_gain_two])
        grad_bias_rows = jnp.stack(
            [
                grad_bias_one,
                jnp.sum(grad_mixed, axis=0),
                grad_bias_two,
                jnp.sum(grad_result, axis=0),
            ]
        )
        grad_parts = (
            grad_wqkv,
            grad_bqv,
            grad_wout,
            grad_wup,
            grad_bup,
            grad_wdown,
            grad_gain_rows,
            grad_bias_rows,
        )
        return (grad_parts, grad_inputs)

    def step(totals, step_items):
        inputs, clip_row, cot_rows = step_items
        front_weights = fetch_weights(w_qkv, b_qv, w_out, w_up, b_up, w_down, gains, biases)
        kept_state, result = forward_pass(inputs, clip_row, front_weights)
        fenced = lax.optimization_barrier(
            (w_qkv, b_qv, w_out, w_up, b_up, w_down, gains, biases, result)
        )
        behind = fetch_weights(
            fenced[0], fenced[1], fenced[2], fenced[3], fenced[4], fenced[5], fenced[6], fenced[7]
        )
        grad_parts, grad_inputs = backward_pass(kept_state, cot_rows, behind)
        totals = tuple((running + grad_part for running, grad_part in zip(totals, grad_parts)))
        return (totals, (result.astype(jnp.bfloat16), grad_inputs))

    zeros_start = (
        jnp.zeros((D, 3, width_local), jnp.float32),
        jnp.zeros((2, 1, width_local), jnp.float32),
        jnp.zeros((width_local, D), jnp.float32),
        jnp.zeros((D, ff_local), jnp.float32),
        jnp.zeros((1, ff_local), jnp.float32),
        jnp.zeros((ff_local, D), jnp.float32),
        jnp.zeros((2, D), jnp.float32),
        jnp.zeros((4, D), jnp.float32),
    )
    totals, (output, frames_grad) = lax.scan(step, zeros_start, (frames, clip_ids, cotangent))
    owned = (
        lax.psum_scatter(totals[0], "dp", scatter_dimension=0, tiled=True),
        lax.psum_scatter(totals[1], "dp", scatter_dimension=2, tiled=True),
        lax.psum_scatter(totals[2], "dp", scatter_dimension=1, tiled=True),
        lax.psum_scatter(totals[3], "dp", scatter_dimension=0, tiled=True),
        lax.psum_scatter(totals[4], "dp", scatter_dimension=1, tiled=True),
        lax.psum_scatter(totals[5], "dp", scatter_dimension=1, tiled=True),
    )
    owned_norms = (
        lax.psum_scatter(totals[6], ("dp", "mp"), scatter_dimension=1, tiled=True),
        lax.psum_scatter(totals[7], ("dp", "mp"), scatter_dimension=1, tiled=True),
    )
    return (
        output,
        frames_grad,
        owned[0],
        owned[1],
        owned[2],
        owned[3],
        owned[4],
        owned[5],
        owned_norms[0],
        owned_norms[1],
    )


def solution(mesh):
    placed = (
        P(None, ("dp", "mp"), None),
        P(),
        P("dp", None, "mp"),
        P(None, "mp", "dp"),
        P("mp", "dp"),
        P("dp", "mp"),
        P("mp", "dp"),
        P("mp", "dp"),
        P(None, ("dp", "mp")),
        P(None, ("dp", "mp")),
        P(None, ("dp", "mp"), None),
    )
    return jax.shard_map(
        local,
        mesh=mesh,
        in_specs=placed,
        out_specs=(
            P(None, ("dp", "mp"), None),
            P(None, ("dp", "mp"), None),
            P("dp", None, "mp"),
            P(None, "mp", "dp"),
            P("mp", "dp"),
            P("dp", "mp"),
            P("mp", "dp"),
            P("mp", "dp"),
            P(None, ("dp", "mp")),
            P(None, ("dp", "mp")),
        ),
        check_vma=False,
    )
```

profile of v0, /device:TPU:0, one launch (start us, length us, event | category | flops | bytes accessed | tf_op | source)
XLA Modules:
  0.0 3567.8 jit_solution(23908522268389208)
XLA Ops:
  9.8 3200.0 %while.31 = (s32[]{:T(128)}, f32[768,3,192]{0,2,1:T(8,128)}, f32[2,1,192]{2,1,0:T(1,128)}, f32[192,768]{1,0:T(8,128)}, f32[768,768]{1,0:T(8,128)}, /*index=5*/f3...) while((s32[]{:T(128)}, f32[768,3,192]{0,2,1:T(8,128)}, ...), condition=%wide.region_31.32_spmd.clone.clone.clone, body=%wide.region_0.31_spmd.clone.clone.clone.sunk | while | flops 11638805504 | bytes 781726784 | solution.py:339
  12.4 43.5 %all-gather.21 = bf16[32,24,2]{1,2,0:T(2,128)(2,1)S(1)} all-gather(bf16[1,24,2]{1,2,0:T(2,128)(2,1)} %bitcast.337), channel_id=1, replica_groups=mesh['dp'=8,'mp'=4] {'dp','mp'}, dimensions={0}, use_global_device_ids=true | all-gather | bytes 3168 | tf_op jit(solution)/shard_map/while/body/eval_jaxpr/all_gather | solution.py:44
  56.1 37.0 %all-gather.20 = bf16[32,24,4]{1,2,0:T(4,128)(2,1)S(1)} all-gather(bf16[1,24,4]{1,2,0:T(4,128)(2,1)} %bitcast.340), channel_id=1, replica_groups=mesh['dp'=8,'mp'=4] {'dp','mp'}, dimensions={0}, use_global_device_ids=true | all-gather | bytes 6336 | tf_op jit(solution)/shard_map/while/body/eval_jaxpr/all_gather | solution.py:45
  93.4 30.6 all_gather.101
  136.7 37.0 %all_gather.99 = bf16[768,3,192]{2,1,0:T(4,128)(2,1)S(1)} all-gather(bf16[96,3,192]{2,1,0:T(4,128)(2,1)S(1)} %copy.86), channel_id=1, replica_groups=mesh['dp'=8,'mp'=4] {'dp'}, dimensions={0}, use_global_device_ids=true | all-gather | bytes 995328 | tf_op jit(solution)/shard_map/while/body/eval_jaxpr/all_gather | solution.py:36
  194.2 22.7 gather_fusion
  216.9 33.2 all_gather.102
  314.0 23.7 all-reduce.9
  368.2 34.0 all-gather.31.cloned.1.call-done
  405.7 22.3 reduce-scatter.29.cloned.1.call-done
  440.5 30.7 all-gather.33.cloned.1.call-done
  476.7 36.6 %all-gather.35.cloned.1.call-done = bf16[768,768]{1,0:T(8,128)(2,1)} async-done(((bf16[96,768]{1,0:T(8,128)(2,1)}), bf16[768,768]{1,0:T(8,128)(2,1)}) %all-gather.35.cloned.1.call-update) | async-done | bytes 1179664 | tf_op jit(solution)/shard_map/while/body/eval_jaxpr/all_gather | solution.py:39
  521.3 38.9 %all-gather.23 = bf16[32,24,2]{1,2,0:T(2,128)(2,1)S(1)} all-gather(bf16[1,24,2]{1,2,0:T(2,128)(2,1)S(1)} %bitcast.338), channel_id=1, replica_groups=mesh['dp'=8,'mp'=4] {'dp','mp'}, dimensions={0}, use_global_device_ids=true | all-gather | bytes 3168 | tf_op jit(solution)/shard_map/while/body/eval_jaxpr/all_gather | solution.py:44
  560.5 33.6 all_gather.109
  594.1 37.0 %all_gather.110 = bf16[768,3,192]{2,0,1:T(8,128)(2,1)} all-gather(bf16[96,3,192]{2,0,1:T(8,128)(2,1)S(1)} %copy-done.32), channel_id=1, replica_groups=mesh['dp'=8,'mp'=4] {'dp'}, dimensions={0}, use_global_device_ids=true | all-gather | bytes 995328 | tf_op jit(solution)/shard_map/while/body/eval_jaxpr/all_gather | solution.py:36
  769.8 35.0 reduce-scatter.33.cloned.1.call-done
  812.0 40.7 %all-gather.21 = bf16[32,24,2]{1,2,0:T(2,128)(2,1)S(1)} all-gather(bf16[1,24,2]{1,2,0:T(2,128)(2,1)} %bitcast.337), channel_id=1, replica_groups=mesh['dp'=8,'mp'=4] {'dp','mp'}, dimensions={0}, use_global_device_ids=true | all-gather | bytes 3168 | tf_op jit(solution)/shard_map/while/body/eval_jaxpr/all_gather | solution.py:44
  853.0 37.0 %all-gather.20 = bf16[32,24,4]{1,2,0:T(4,128)(2,1)S(1)} all-gather(bf16[1,24,4]{1,2,0:T(4,128)(2,1)} %bitcast.340), channel_id=1, replica_groups=mesh['dp'=8,'mp'=4] {'dp','mp'}, dimensions={0}, use_global_device_ids=true | all-gather | bytes 6336 | tf_op jit(solution)/shard_map/while/body/eval_jaxpr/all_gather | solution.py:45
  890.3 30.6 all_gather.101
  933.5 37.0 %all_gather.99 = bf16[768,3,192]{2,1,0:T(4,128)(2,1)S(1)} all-gather(bf16[96,3,192]{2,1,0:T(4,128)(2,1)S(1)} %copy.86), channel_id=1, replica_groups=mesh['dp'=8,'mp'=4] {'dp'}, dimensions={0}, use_global_device_ids=true | all-gather | bytes 995328 | tf_op jit(solution)/shard_map/while/body/eval_jaxpr/all_gather | solution.py:36
  991.0 22.7 gather_fusion
  1013.8 33.2 all_gather.102
  1110.7 23.7 all-reduce.9
  1165.0 34.3 all-gather.31.cloned.1.call-done
  1237.4 30.9 all-gather.33.cloned.1.call-done
  1273.7 36.4 %all-gather.35.cloned.1.call-done = bf16[768,768]{1,0:T(8,128)(2,1)} async-done(((bf16[96,768]{1,0:T(8,128)(2,1)}), bf16[768,768]{1,0:T(8,128)(2,1)}) %all-gather.35.cloned.1.call-update) | async-done | bytes 1179664 | tf_op jit(solution)/shard_map/while/body/eval_jaxpr/all_gather | solution.py:39
  1318.9 38.9 %all-gather.23 = bf16[32,24,2]{1,2,0:T(2,128)(2,1)S(1)} all-gather(bf16[1,24,2]{1,2,0:T(2,128)(2,1)S(1)} %bitcast.338), channel_id=1, replica_groups=mesh['dp'=8,'mp'=4] {'dp','mp'}, dimensions={0}, use_global_device_ids=true | all-gather | bytes 3168 | tf_op jit(solution)/shard_map/while/body/eval_jaxpr/all_gather | solution.py:44
  1358.1 33.6 all_gather.109
  1391.7 37.0 %all_gather.110 = bf16[768,3,192]{2,0,1:T(8,128)(2,1)} all-gather(bf16[96,3,192]{2,0,1:T(8,128)(2,1)S(1)} %copy-done.32), channel_id=1, replica_groups=mesh['dp'=8,'mp'=4] {'dp'}, dimensions={0}, use_global_device_ids=true | all-gather | bytes 995328 | tf_op jit(solution)/shard_map/while/body/eval_jaxpr/all_gather | solution.py:36
  1570.9 33.2 reduce-scatter.33.cloned.1.call-done
  1611.3 40.7 %all-gather.21 = bf16[32,24,2]{1,2,0:T(2,128)(2,1)S(1)} all-gather(bf16[1,24,2]{1,2,0:T(2,128)(2,1)} %bitcast.337), channel_id=1, replica_groups=mesh['dp'=8,'mp'=4] {'dp','mp'}, dimensions={0}, use_global_device_ids=true | all-gather | bytes 3168 | tf_op jit(solution)/shard_map/while/body/eval_jaxpr/all_gather | solution.py:44
  1652.4 37.0 %all-gather.20 = bf16[32,24,4]{1,2,0:T(4,128)(2,1)S(1)} all-gather(bf16[1,24,4]{1,2,0:T(4,128)(2,1)} %bitcast.340), channel_id=1, replica_groups=mesh['dp'=8,'mp'=4] {'dp','mp'}, dimensions={0}, use_global_device_ids=true | all-gather | bytes 6336 | tf_op jit(solution)/shard_map/while/body/eval_jaxpr/all_gather | solution.py:45
  1689.7 30.6 all_gather.101
  1732.9 37.0 %all_gather.99 = bf16[768,3,192]{2,1,0:T(4,128)(2,1)S(1)} all-gather(bf16[96,3,192]{2,1,0:T(4,128)(2,1)S(1)} %copy.86), channel_id=1, replica_groups=mesh['dp'=8,'mp'=4] {'dp'}, dimensions={0}, use_global_device_ids=true | all-gather | bytes 995328 | tf_op jit(solution)/shard_map/while/body/eval_jaxpr/all_gather | solution.py:36
  1790.4 22.7 gather_fusion
  1813.1 33.2 all_gather.102
  1909.9 23.8 all-reduce.9
  1964.2 34.1 all-gather.31.cloned.1.call-done
  2036.6 30.7 all-gather.33.cloned.1.call-done
  2072.8 36.6 %all-gather.35.cloned.1.call-done = bf16[768,768]{1,0:T(8,128)(2,1)} async-done(((bf16[96,768]{1,0:T(8,128)(2,1)}), bf16[768,768]{1,0:T(8,128)(2,1)}) %all-gather.35.cloned.1.call-update) | async-done | bytes 1179664 | tf_op jit(solution)/shard_map/while/body/eval_jaxpr/all_gather | solution.py:39
  2118.2 38.9 %all-gather.23 = bf16[32,24,2]{1,2,0:T(2,128)(2,1)S(1)} all-gather(bf16[1,24,2]{1,2,0:T(2,128)(2,1)S(1)} %bitcast.338), channel_id=1, replica_groups=mesh['dp'=8,'mp'=4] {'dp','mp'}, dimensions={0}, use_global_device_ids=true | all-gather | bytes 3168 | tf_op jit(solution)/shard_map/while/body/eval_jaxpr/all_gather | solution.py:44
  2157.4 33.6 all_gather.109
  2191.0 37.0 %all_gather.110 = bf16[768,3,192]{2,0,1:T(8,128)(2,1)} all-gather(bf16[96,3,192]{2,0,1:T(8,128)(2,1)S(1)} %copy-done.32), channel_id=1, replica_groups=mesh['dp'=8,'mp'=4] {'dp'}, dimensions={0}, use_global_device_ids=true | all-gather | bytes 995328 | tf_op jit(solution)/shard_map/while/body/eval_jaxpr/all_gather | solution.py:36
  2370.2 33.2 reduce-scatter.33.cloned.1.call-done
  2410.6 40.7 %all-gather.21 = bf16[32,24,2]{1,2,0:T(2,128)(2,1)S(1)} all-gather(bf16[1,24,2]{1,2,0:T(2,128)(2,1)} %bitcast.337), channel_id=1, replica_groups=mesh['dp'=8,'mp'=4] {'dp','mp'}, dimensions={0}, use_global_device_ids=true | all-gather | bytes 3168 | tf_op jit(solution)/shard_map/while/body/eval_jaxpr/all_gather | solution.py:44
  2451.6 37.0 %all-gather.20 = bf16[32,24,4]{1,2,0:T(4,128)(2,1)S(1)} all-gather(bf16[1,24,4]{1,2,0:T(4,128)(2,1)} %bitcast.340), channel_id=1, replica_groups=mesh['dp'=8,'mp'=4] {'dp','mp'}, dimensions={0}, use_global_device_ids=true | all-gather | bytes 6336 | tf_op jit(solution)/shard_map/while/body/eval_jaxpr/all_gather | solution.py:45
  2488.9 30.6 all_gather.101
  2532.2 37.0 %all_gather.99 = bf16[768,3,192]{2,1,0:T(4,128)(2,1)S(1)} all-gather(bf16[96,3,192]{2,1,0:T(4,128)(2,1)S(1)} %copy.86), channel_id=1, replica_groups=mesh['dp'=8,'mp'=4] {'dp'}, dimensions={0}, use_global_device_ids=true | all-gather | bytes 995328 | tf_op jit(solution)/shard_map/while/body/eval_jaxpr/all_gather | solution.py:36
  2589.7 22.7 gather_fusion
  2612.4 33.2 all_gather.102
  2709.2 23.8 all-reduce.9
  2763.4 34.1 all-gather.31.cloned.1.call-done
  2801.0 22.3 reduce-scatter.29.cloned.1.call-done
  2835.8 30.7 all-gather.33.cloned.1.call-done
  2872.0 36.6 %all-gather.35.cloned.1.call-done = bf16[768,768]{1,0:T(8,128)(2,1)} async-done(((bf16[96,768]{1,0:T(8,128)(2,1)}), bf16[768,768]{1,0:T(8,128)(2,1)}) %all-gather.35.cloned.1.call-update) | async-done | bytes 1179664 | tf_op jit(solution)/shard_map/while/body/eval_jaxpr/all_gather | solution.py:39
  2917.4 38.9 %all-gather.23 = bf16[32,24,2]{1,2,0:T(2,128)(2,1)S(1)} all-gather(bf16[1,24,2]{1,2,0:T(2,128)(2,1)S(1)} %bitcast.338), channel_id=1, replica_groups=mesh['dp'=8,'mp'=4] {'dp','mp'}, dimensions={0}, use_global_device_ids=true | all-gather | bytes 3168 | tf_op jit(solution)/shard_map/while/body/eval_jaxpr/all_gather | solution.py:44
  2956.6 33.6 all_gather.109
  2990.2 37.0 %all_gather.110 = bf16[768,3,192]{2,0,1:T(8,128)(2,1)} all-gather(bf16[96,3,192]{2,0,1:T(8,128)(2,1)S(1)} %copy-done.32), channel_id=1, replica_groups=mesh['dp'=8,'mp'=4] {'dp'}, dimensions={0}, use_global_device_ids=true | all-gather | bytes 995328 | tf_op jit(solution)/shard_map/while/body/eval_jaxpr/all_gather | solution.py:36
  3169.3 33.2 reduce-scatter.33.cloned.1.call-done
  3243.7 37.3 %all-reduce.7 = (f32[2,768]{1,0:T(2,128)S(1)}, f32[4,768]{1,0:T(4,128)S(1)}) all-reduce(f32[2,768]{1,0:T(2,128)S(1)} %copy-done.55, f32[4,768]{1,0:T(4,128)S(1)} %copy-done.42), channel_id=13, replica_groups=mesh['dp'=8,'mp'=4] {'dp','mp'}, use_global_device_ids=true, to_apply=%region_38.39.clone | all-reduce | flops 4608 | bytes 36864
  3284.4 56.9 %reduce-scatter.23.cloned.1.call-done = f32[96,192]{1,0:T(8,128)} async-done(((f32[768,192]{1,0:T(8,128)}), f32[96,192]{1,0:T(8,128)}) %reduce-scatter.23.cloned.1.call-update) | async-done | bytes 73744
  3342.9 71.2 %reduce-scatter.17.cloned.1.call-done = f32[96,3,192]{2,0,1:T(8,128)} async-done(((f32[768,3,192]{2,0,1:T(8,128)}), f32[96,3,192]{2,0,1:T(8,128)}) %reduce-scatter.17.cloned.1.call-update) | async-done | bytes 221200 | tf_op jit(solution)/shard_map/reduce_scatter | solution.py:341
  3414.1 72.8 %reduce-scatter.19.cloned.1.call-done = f32[96,768]{1,0:T(8,128)} async-done(((f32[768,768]{1,0:T(8,128)}), f32[96,768]{1,0:T(8,128)}) %reduce-scatter.19.cloned.1.call-update) | async-done | bytes 294928 | tf_op jit(solution)/shard_map/reduce_scatter | solution.py:344
  3486.8 73.1 %reduce-scatter.21.cloned.1.call-done = f32[768,96]{0,1:T(8,128)} async-done(((f32[768,768]{0,1:T(8,128)}), f32[768,96]{0,1:T(8,128)}) %reduce-scatter.21.cloned.1.call-update) | async-done | bytes 294928 | tf_op jit(solution)/shard_map/reduce_scatter | solution.py:346
  (1362 shorter events, 1301.9 us)
Async XLA Ops:
  10.1 330.3 %reduce-scatter.27.cloned.1.call-start = ((), (), s32[]{:S(2)}) async-start(), calls=%async_computation.14 | async-start | bytes 1105920 | tf_op jit(solution)/shard_map/while/body/eval_jaxpr/reduce_scatter | solution.py:64
  175.7 74.5 %collective-permute-start.5 = (bf16[576,2,192]{0,2,1:T(8,128)(2,1)S(1)}, bf16[576,2,192]{0,2,1:T(8,128)(2,1)S(1)}, u32[]{:S(2)}, u32[]{:S(2)}) collective-permute-start(bf16[576,2,192]{0,2,1:T(8,128)(2,1)S(1)} %slice.463), channel_id=1, source_target_pairs={{12,0},{16,4},{20,8},{24,12},{28,16},{13,1},{17,5},{21,9},{25,13},... | collective-permute-start | bytes 1327112 | tf_op jit(solution)/shard_map/while/body/eval_jaxpr/ppermute | solution.py:16
  177.0 77.0 %collective-permute-start.4 = (bf16[576,2,192]{0,2,1:T(8,128)(2,1)S(1)}, bf16[576,2,192]{0,2,1:T(8,128)(2,1)S(1)}, u32[]{:S(2)}, u32[]{:S(2)}) collective-permute-start(bf16[576,2,192]{0,2,1:T(8,128)(2,1)S(1)} %slice.463), channel_id=1, source_target_pairs={{8,0},{12,4},{16,8},{20,12},{24,16},{28,20},{9,1},{13,5},{17,9},{2... | collective-permute-start | bytes 1327112 | tf_op jit(solution)/shard_map/while/body/eval_jaxpr/ppermute | solution.py:16
  178.3 75.7 %collective-permute-start.3 = (bf16[576,2,192]{0,2,1:T(8,128)(2,1)S(1)}, bf16[576,2,192]{0,2,1:T(8,128)(2,1)S(1)}, u32[]{:S(2)}, u32[]{:S(2)}) collective-permute-start(bf16[576,2,192]{0,2,1:T(8,128)(2,1)S(1)} %slice.463), channel_id=1, source_target_pairs={{4,0},{8,4},{12,8},{16,12},{20,16},{24,20},{28,24},{5,1},{9,5},{13... | collective-permute-start | bytes 1327112 | tf_op jit(solution)/shard_map/while/body/eval_jaxpr/ppermute | solution.py:16
  179.6 74.4 %collective-permute-start.2 = (bf16[576,2,192]{0,2,1:T(8,128)(2,1)S(1)}, bf16[576,2,192]{0,2,1:T(8,128)(2,1)}, u32[]{:S(2)}, u32[]{:S(2)}) collective-permute-start(bf16[576,2,192]{0,2,1:T(8,128)(2,1)S(1)} %slice.463), channel_id=1, source_target_pairs={{0,4},{4,8},{8,12},{12,16},{16,20},{20,24},{24,28},{1,5},{5,9},{9,... | collective-permute-start | bytes 1327112 | tf_op jit(solution)/shard_map/while/body/eval_jaxpr/ppermute | solution.py:16
  184.9 69.1 %collective-permute-start.1 = (bf16[576,2,192]{0,2,1:T(8,128)(2,1)S(1)}, bf16[576,2,192]{0,2,1:T(8,128)(2,1)}, u32[]{:S(2)}, u32[]{:S(2)}) collective-permute-start(bf16[576,2,192]{0,2,1:T(8,128)(2,1)S(1)} %slice.463), channel_id=1, source_target_pairs={{0,8},{4,12},{8,16},{12,20},{16,24},{20,28},{1,9},{5,13},{9,17},{1... | collective-permute-start | bytes 1327112 | tf_op jit(solution)/shard_map/while/body/eval_jaxpr/ppermute | solution.py:16
  311.2 49.1 %all-gather.29.cloned.1.call-start = ((), (), s32[]{:S(2)}) async-start(), calls=%async_computation.15 | async-start | bytes 1327104 | tf_op jit(solution)/shard_map/while/body/eval_jaxpr/all_gather | solution.py:39
  311.8 90.4 %all-gather.31.cloned.1.call-start = ((), (), s32[]{:S(2)}) async-start(), calls=%async_computation.16 | async-start | bytes 1327104 | tf_op jit(solution)/shard_map/while/body/eval_jaxpr/all_gather | solution.py:41
  312.4 115.5 %reduce-scatter.29.cloned.1.call-start = ((), (), s32[]{:S(2)}) async-start(), calls=%async_computation.17 | async-start | bytes 1105920 | tf_op jit(solution)/shard_map/while/body/eval_jaxpr/reduce_scatter | solution.py:64
  405.6 65.6 %all-gather.33.cloned.1.call-start = ((), (), s32[]{:S(2)}) async-start(), calls=%async_computation.18 | async-start | bytes 1327104 | tf_op jit(solution)/shard_map/while/body/eval_jaxpr/all_gather | solution.py:41
  429.7 83.5 %all-gather.35.cloned.1.call-start = ((), (), s32[]{:S(2)}) async-start(), calls=%async_computation.19 | async-start | bytes 1327104 | tf_op jit(solution)/shard_map/while/body/eval_jaxpr/all_gather | solution.py:39
  430.4 203.3 %reduce-scatter.31.cloned.1.call-start = ((), (), s32[]{:S(2)}) async-start(), calls=%async_computation.20 | async-start | bytes 1105920 | tf_op jit(solution)/shard_map/while/body/eval_jaxpr/reduce_scatter | solution.py:80
  516.6 288.1 %reduce-scatter.33.cloned.1.call-start = ((), (), s32[]{:S(2)}) async-start(), calls=%async_computation.21 | async-start | bytes 1105920 | tf_op jit(solution)/shard_map/while/body/eval_jaxpr/reduce_scatter | solution.py:80
  726.9 26.6 collective-permute-start.8
  736.8 24.0 collective-permute-start.11
  809.7 327.2 %reduce-scatter.27.cloned.1.call-start = ((), (), s32[]{:S(2)}) async-start(), calls=%async_computation.14 | async-start | bytes 1105920 | tf_op jit(solution)/shard_map/while/body/eval_jaxpr/reduce_scatter | solution.py:64
  972.6 74.5 %collective-permute-start.5 = (bf16[576,2,192]{0,2,1:T(8,128)(2,1)S(1)}, bf16[576,2,192]{0,2,1:T(8,128)(2,1)S(1)}, u32[]{:S(2)}, u32[]{:S(2)}) collective-permute-start(bf16[576,2,192]{0,2,1:T(8,128)(2,1)S(1)} %slice.463), channel_id=1, source_target_pairs={{12,0},{16,4},{20,8},{24,12},{28,16},{13,1},{17,5},{21,9},{25,13},... | collective-permute-start | bytes 1327112 | tf_op jit(solution)/shard_map/while/body/eval_jaxpr/ppermute | solution.py:16
  973.9 77.0 %collective-permute-start.4 = (bf16[576,2,192]{0,2,1:T(8,128)(2,1)S(1)}, bf16[576,2,192]{0,2,1:T(8,128)(2,1)S(1)}, u32[]{:S(2)}, u32[]{:S(2)}) collective-permute-start(bf16[576,2,192]{0,2,1:T(8,128)(2,1)S(1)} %slice.463), channel_id=1, source_target_pairs={{8,0},{12,4},{16,8},{20,12},{24,16},{28,20},{9,1},{13,5},{17,9},{2... | collective-permute-start | bytes 1327112 | tf_op jit(solution)/shard_map/while/body/eval_jaxpr/ppermute | solution.py:16
  975.2 75.7 %collective-permute-start.3 = (bf16[576,2,192]{0,2,1:T(8,128)(2,1)S(1)}, bf16[576,2,192]{0,2,1:T(8,128)(2,1)S(1)}, u32[]{:S(2)}, u32[]{:S(2)}) collective-permute-start(bf16[576,2,192]{0,2,1:T(8,128)(2,1)S(1)} %slice.463), channel_id=1, source_target_pairs={{4,0},{8,4},{12,8},{16,12},{20,16},{24,20},{28,24},{5,1},{9,5},{13... | collective-permute-start | bytes 1327112 | tf_op jit(solution)/shard_map/while/body/eval_jaxpr/ppermute | solution.py:16
  976.5 74.4 %collective-permute-start.2 = (bf16[576,2,192]{0,2,1:T(8,128)(2,1)S(1)}, bf16[576,2,192]{0,2,1:T(8,128)(2,1)}, u32[]{:S(2)}, u32[]{:S(2)}) collective-permute-start(bf16[576,2,192]{0,2,1:T(8,128)(2,1)S(1)} %slice.463), channel_id=1, source_target_pairs={{0,4},{4,8},{8,12},{12,16},{16,20},{20,24},{24,28},{1,5},{5,9},{9,... | collective-permute-start | bytes 1327112 | tf_op jit(solution)/shard_map/while/body/eval_jaxpr/ppermute | solution.py:16
  981.8 69.1 %collective-permute-start.1 = (bf16[576,2,192]{0,2,1:T(8,128)(2,1)S(1)}, bf16[576,2,192]{0,2,1:T(8,128)(2,1)}, u32[]{:S(2)}, u32[]{:S(2)}) collective-permute-start(bf16[576,2,192]{0,2,1:T(8,128)(2,1)S(1)} %slice.463), channel_id=1, source_target_pairs={{0,8},{4,12},{8,16},{12,20},{16,24},{20,28},{1,9},{5,13},{9,17},{1... | collective-permute-start | bytes 1327112 | tf_op jit(solution)/shard_map/while/body/eval_jaxpr/ppermute | solution.py:16
  1107.7 49.4 %all-gather.29.cloned.1.call-start = ((), (), s32[]{:S(2)}) async-start(), calls=%async_computation.15 | async-start | bytes 1327104 | tf_op jit(solution)/shard_map/while/body/eval_jaxpr/all_gather | solution.py:39
  1108.4 90.8 %all-gather.31.cloned.1.call-start = ((), (), s32[]{:S(2)}) async-start(), calls=%async_computation.16 | async-start | bytes 1327104 | tf_op jit(solution)/shard_map/while/body/eval_jaxpr/all_gather | solution.py:41
  1109.2 115.8 %reduce-scatter.29.cloned.1.call-start = ((), (), s32[]{:S(2)}) async-start(), calls=%async_computation.17 | async-start | bytes 1105920 | tf_op jit(solution)/shard_map/while/body/eval_jaxpr/reduce_scatter | solution.py:64
  1202.7 65.6 %all-gather.33.cloned.1.call-start = ((), (), s32[]{:S(2)}) async-start(), calls=%async_computation.18 | async-start | bytes 1327104 | tf_op jit(solution)/shard_map/while/body/eval_jaxpr/all_gather | solution.py:41
  1226.7 83.4 %all-gather.35.cloned.1.call-start = ((), (), s32[]{:S(2)}) async-start(), calls=%async_computation.19 | async-start | bytes 1327104 | tf_op jit(solution)/shard_map/while/body/eval_jaxpr/all_gather | solution.py:39
  1227.3 205.7 %reduce-scatter.31.cloned.1.call-start = ((), (), s32[]{:S(2)}) async-start(), calls=%async_computation.20 | async-start | bytes 1105920 | tf_op jit(solution)/shard_map/while/body/eval_jaxpr/reduce_scatter | solution.py:80
  1313.5 290.6 %reduce-scatter.33.cloned.1.call-start = ((), (), s32[]{:S(2)}) async-start(), calls=%async_computation.21 | async-start | bytes 1105920 | tf_op jit(solution)/shard_map/while/body/eval_jaxpr/reduce_scatter | solution.py:80
  1526.3 26.6 collective-permute-start.8
  1609.0 327.2 %reduce-scatter.27.cloned.1.call-start = ((), (), s32[]{:S(2)}) async-start(), calls=%async_computation.14 | async-start | bytes 1105920 | tf_op jit(solution)/shard_map/while/body/eval_jaxpr/reduce_scatter | solution.py:64
  1771.9 74.5 %collective-permute-start.5 = (bf16[576,2,192]{0,2,1:T(8,128)(2,1)S(1)}, bf16[576,2,192]{0,2,1:T(8,128)(2,1)S(1)}, u32[]{:S(2)}, u32[]{:S(2)}) collective-permute-start(bf16[576,2,192]{0,2,1:T(8,128)(2,1)S(1)} %slice.463), channel_id=1, source_target_pairs={{12,0},{16,4},{20,8},{24,12},{28,16},{13,1},{17,5},{21,9},{25,13},... | collective-permute-start | bytes 1327112 | tf_op jit(solution)/shard_map/while/body/eval_jaxpr/ppermute | solution.py:16
  1773.2 77.0 %collective-permute-start.4 = (bf16[576,2,192]{0,2,1:T(8,128)(2,1)S(1)}, bf16[576,2,192]{0,2,1:T(8,128)(2,1)S(1)}, u32[]{:S(2)}, u32[]{:S(2)}) collective-permute-start(bf16[576,2,192]{0,2,1:T(8,128)(2,1)S(1)} %slice.463), channel_id=1, source_target_pairs={{8,0},{12,4},{16,8},{20,12},{24,16},{28,20},{9,1},{13,5},{17,9},{2... | collective-permute-start | bytes 1327112 | tf_op jit(solution)/shard_map/while/body/eval_jaxpr/ppermute | solution.py:16
  1774.5 75.7 %collective-permute-start.3 = (bf16[576,2,192]{0,2,1:T(8,128)(2,1)S(1)}, bf16[576,2,192]{0,2,1:T(8,128)(2,1)S(1)}, u32[]{:S(2)}, u32[]{:S(2)}) collective-permute-start(bf16[576,2,192]{0,2,1:T(8,128)(2,1)S(1)} %slice.463), channel_id=1, source_target_pairs={{4,0},{8,4},{12,8},{16,12},{20,16},{24,20},{28,24},{5,1},{9,5},{13... | collective-permute-start | bytes 1327112 | tf_op jit(solution)/shard_map/while/body/eval_jaxpr/ppermute | solution.py:16
  1775.8 74.4 %collective-permute-start.2 = (bf16[576,2,192]{0,2,1:T(8,128)(2,1)S(1)}, bf16[576,2,192]{0,2,1:T(8,128)(2,1)}, u32[]{:S(2)}, u32[]{:S(2)}) collective-permute-start(bf16[576,2,192]{0,2,1:T(8,128)(2,1)S(1)} %slice.463), channel_id=1, source_target_pairs={{0,4},{4,8},{8,12},{12,16},{16,20},{20,24},{24,28},{1,5},{5,9},{9,... | collective-permute-start | bytes 1327112 | tf_op jit(solution)/shard_map/while/body/eval_jaxpr/ppermute | solution.py:16
  1781.1 69.1 %collective-permute-start.1 = (bf16[576,2,192]{0,2,1:T(8,128)(2,1)S(1)}, bf16[576,2,192]{0,2,1:T(8,128)(2,1)}, u32[]{:S(2)}, u32[]{:S(2)}) collective-permute-start(bf16[576,2,192]{0,2,1:T(8,128)(2,1)S(1)} %slice.463), channel_id=1, source_target_pairs={{0,8},{4,12},{8,16},{12,20},{16,24},{20,28},{1,9},{5,13},{9,17},{1... | collective-permute-start | bytes 1327112 | tf_op jit(solution)/shard_map/while/body/eval_jaxpr/ppermute | solution.py:16
  1907.0 49.3 %all-gather.29.cloned.1.call-start = ((), (), s32[]{:S(2)}) async-start(), calls=%async_computation.15 | async-start | bytes 1327104 | tf_op jit(solution)/shard_map/while/body/eval_jaxpr/all_gather | solution.py:39
  1907.6 90.7 %all-gather.31.cloned.1.call-start = ((), (), s32[]{:S(2)}) async-start(), calls=%async_computation.16 | async-start | bytes 1327104 | tf_op jit(solution)/shard_map/while/body/eval_jaxpr/all_gather | solution.py:41
  1908.4 115.7 %reduce-scatter.29.cloned.1.call-start = ((), (), s32[]{:S(2)}) async-start(), calls=%async_computation.17 | async-start | bytes 1105920 | tf_op jit(solution)/shard_map/while/body/eval_jaxpr/reduce_scatter | solution.py:64
  2001.7 65.6 %all-gather.33.cloned.1.call-start = ((), (), s32[]{:S(2)}) async-start(), calls=%async_computation.18 | async-start | bytes 1327104 | tf_op jit(solution)/shard_map/while/body/eval_jaxpr/all_gather | solution.py:41
  2025.8 83.5 %all-gather.35.cloned.1.call-start = ((), (), s32[]{:S(2)}) async-start(), calls=%async_computation.19 | async-start | bytes 1327104 | tf_op jit(solution)/shard_map/while/body/eval_jaxpr/all_gather | solution.py:39
  2026.6 205.7 %reduce-scatter.31.cloned.1.call-start = ((), (), s32[]{:S(2)}) async-start(), calls=%async_computation.20 | async-start | bytes 1105920 | tf_op jit(solution)/shard_map/while/body/eval_jaxpr/reduce_scatter | solution.py:80
  2112.7 290.6 %reduce-scatter.33.cloned.1.call-start = ((), (), s32[]{:S(2)}) async-start(), calls=%async_computation.21 | async-start | bytes 1105920 | tf_op jit(solution)/shard_map/while/body/eval_jaxpr/reduce_scatter | solution.py:80
  2325.6 26.6 collective-permute-start.8
  2335.5 24.0 collective-permute-start.11
  2408.3 327.2 %reduce-scatter.27.cloned.1.call-start = ((), (), s32[]{:S(2)}) async-start(), calls=%async_computation.14 | async-start | bytes 1105920 | tf_op jit(solution)/shard_map/while/body/eval_jaxpr/reduce_scatter | solution.py:64
  2571.2 74.5 %collective-permute-start.5 = (bf16[576,2,192]{0,2,1:T(8,128)(2,1)S(1)}, bf16[576,2,192]{0,2,1:T(8,128)(2,1)S(1)}, u32[]{:S(2)}, u32[]{:S(2)}) collective-permute-start(bf16[576,2,192]{0,2,1:T(8,128)(2,1)S(1)} %slice.463), channel_id=1, source_target_pairs={{12,0},{16,4},{20,8},{24,12},{28,16},{13,1},{17,5},{21,9},{25,13},... | collective-permute-start | bytes 1327112 | tf_op jit(solution)/shard_map/while/body/eval_jaxpr/ppermute | solution.py:16
  2572.5 77.0 %collective-permute-start.4 = (bf16[576,2,192]{0,2,1:T(8,128)(2,1)S(1)}, bf16[576,2,192]{0,2,1:T(8,128)(2,1)S(1)}, u32[]{:S(2)}, u32[]{:S(2)}) collective-permute-start(bf16[576,2,192]{0,2,1:T(8,128)(2,1)S(1)} %slice.463), channel_id=1, source_target_pairs={{8,0},{12,4},{16,8},{20,12},{24,16},{28,20},{9,1},{13,5},{17,9},{2... | collective-permute-start | bytes 1327112 | tf_op jit(solution)/shard_map/while/body/eval_jaxpr/ppermute | solution.py:16
  2573.8 75.7 %collective-permute-start.3 = (bf16[576,2,192]{0,2,1:T(8,128)(2,1)S(1)}, bf16[576,2,192]{0,2,1:T(8,128)(2,1)S(1)}, u32[]{:S(2)}, u32[]{:S(2)}) collective-permute-start(bf16[576,2,192]{0,2,1:T(8,128)(2,1)S(1)} %slice.463), channel_id=1, source_target_pairs={{4,0},{8,4},{12,8},{16,12},{20,16},{24,20},{28,24},{5,1},{9,5},{13... | collective-permute-start | bytes 1327112 | tf_op jit(solution)/shard_map/while/body/eval_jaxpr/ppermute | solution.py:16
  2575.1 74.4 %collective-permute-start.2 = (bf16[576,2,192]{0,2,1:T(8,128)(2,1)S(1)}, bf16[576,2,192]{0,2,1:T(8,128)(2,1)}, u32[]{:S(2)}, u32[]{:S(2)}) collective-permute-start(bf16[576,2,192]{0,2,1:T(8,128)(2,1)S(1)} %slice.463), channel_id=1, source_target_pairs={{0,4},{4,8},{8,12},{12,16},{16,20},{20,24},{24,28},{1,5},{5,9},{9,... | collective-permute-start | bytes 1327112 | tf_op jit(solution)/shard_map/while/body/eval_jaxpr/ppermute | solution.py:16
  2580.4 69.1 %collective-permute-start.1 = (bf16[576,2,192]{0,2,1:T(8,128)(2,1)S(1)}, bf16[576,2,192]{0,2,1:T(8,128)(2,1)}, u32[]{:S(2)}, u32[]{:S(2)}) collective-permute-start(bf16[576,2,192]{0,2,1:T(8,128)(2,1)S(1)} %slice.463), channel_id=1, source_target_pairs={{0,8},{4,12},{8,16},{12,20},{16,24},{20,28},{1,9},{5,13},{9,17},{1... | collective-permute-start | bytes 1327112 | tf_op jit(solution)/shard_map/while/body/eval_jaxpr/ppermute | solution.py:16
  2706.3 49.2 %all-gather.29.cloned.1.call-start = ((), (), s32[]{:S(2)}) async-start(), calls=%async_computation.15 | async-start | bytes 1327104 | tf_op jit(solution)/shard_map/while/body/eval_jaxpr/all_gather | solution.py:39
  2706.9 90.6 %all-gather.31.cloned.1.call-start = ((), (), s32[]{:S(2)}) async-start(), calls=%async_computation.16 | async-start | bytes 1327104 | tf_op jit(solution)/shard_map/while/body/eval_jaxpr/all_gather | solution.py:41
  2707.6 115.6 %reduce-scatter.29.cloned.1.call-start = ((), (), s32[]{:S(2)}) async-start(), calls=%async_computation.17 | async-start | bytes 1105920 | tf_op jit(solution)/shard_map/while/body/eval_jaxpr/reduce_scatter | solution.py:64
  2800.9 65.6 %all-gather.33.cloned.1.call-start = ((), (), s32[]{:S(2)}) async-start(), calls=%async_computation.18 | async-start | bytes 1327104 | tf_op jit(solution)/shard_map/while/body/eval_jaxpr/all_gather | solution.py:41
  2825.0 83.5 %all-gather.35.cloned.1.call-start = ((), (), s32[]{:S(2)}) async-start(), calls=%async_computation.19 | async-start | bytes 1327104 | tf_op jit(solution)/shard_map/while/body/eval_jaxpr/all_gather | solution.py:39
  2825.8 205.7 %reduce-scatter.31.cloned.1.call-start = ((), (), s32[]{:S(2)}) async-start(), calls=%async_computation.20 | async-start | bytes 1105920 | tf_op jit(solution)/shard_map/while/body/eval_jaxpr/reduce_scatter | solution.py:80
  2911.9 290.6 %reduce-scatter.33.cloned.1.call-start = ((), (), s32[]{:S(2)}) async-start(), calls=%async_computation.21 | async-start | bytes 1105920 | tf_op jit(solution)/shard_map/while/body/eval_jaxpr/reduce_scatter | solution.py:80
  3124.7 26.7 collective-permute-start.8
  3134.6 24.0 collective-permute-start.11
  3209.7 73.2 %reduce-scatter.25.cloned.1.call-start = ((), (), s32[]{:S(2)}) async-start(), calls=%async_computation.13 | async-start | bytes 442368
  3211.4 129.8 %reduce-scatter.23.cloned.1.call-start = ((), (), s32[]{:S(2)}) async-start(), calls=%async_computation.12 | async-start | bytes 884736
  3213.7 200.3 %reduce-scatter.17.cloned.1.call-start = ((), (), s32[]{:S(2)}) async-start(), calls=%async_computation.9 | async-start | bytes 2654208 | tf_op jit(solution)/shard_map/reduce_scatter | solution.py:341
  3216.8 270.0 %reduce-scatter.19.cloned.1.call-start = ((), (), s32[]{:S(2)}) async-start(), calls=%async_computation.10 | async-start | bytes 2654208 | tf_op jit(solution)/shard_map/reduce_scatter | solution.py:344
  3217.4 342.6 %reduce-scatter.21.cloned.1.call-start = ((), (), s32[]{:S(2)}) async-start(), calls=%async_computation.11 | async-start | bytes 2654208 | tf_op jit(solution)/shard_map/reduce_scatter | solution.py:346
  (334 other events, 7935.7 us)
Sparse Core Ops, SparseCore 0:
  311.3 29.0 reduce-scatter.26
  405.7 22.1 reduce-scatter.28
  516.7 22.1 reduce-scatter.30
  763.5 41.1 reduce-scatter.32
  1107.8 29.0 reduce-scatter.26
  1202.8 22.1 reduce-scatter.28
  1313.6 22.1 reduce-scatter.30
  1562.9 41.1 reduce-scatter.32
  1907.2 29.0 reduce-scatter.26
  2001.9 22.1 reduce-scatter.28
  2112.9 22.1 reduce-scatter.30
  2362.1 41.1 reduce-scatter.32
  2706.4 29.0 reduce-scatter.26
  2801.1 22.1 reduce-scatter.28
  2912.1 22.1 reduce-scatter.30
  3161.3 41.1 reduce-scatter.32
  3213.5 62.2 reduce-scatter.24
  3278.9 62.2 reduce-scatter.22
  3345.3 68.7 reduce-scatter.16
  3418.0 68.8 reduce-scatter.18
  3490.9 68.9 reduce-scatter.20
Sparse Core Ops, SparseCore 1:
  313.9 46.4 all-gather.28
  362.4 39.7 all-gather.30
  429.8 41.4 all-gather.32
  473.4 39.7 all-gather.34
  1110.7 46.4 all-gather.28
  1159.3 39.9 all-gather.30
  1226.8 41.4 all-gather.32
  1270.3 39.7 all-gather.34
  1909.7 46.5 all-gather.28
  1958.5 39.7 all-gather.30
  2025.9 41.4 all-gather.32
  2069.6 39.7 all-gather.34
  2709.0 46.5 all-gather.28
  2757.7 39.7 all-gather.30
  2825.1 41.4 all-gather.32
  2868.8 39.7 all-gather.34
where the time goes:
time: 3580 us; the launch traced here: 3570 us
  blocking collectives  1450 us (41%)
  waiting for transfers between devices  1050 us (29%)
  matrix products  374 us (10%)
  other arithmetic  347 us (10%)
  local copies, waits for them, and re-layouts  193 us (5%)
  starting transfers between devices  122 us (3%)
    all_gather x8, blocking collectives, fetch_weights(): lax.all_gather(gains, ('dp', 'mp'), axis=1, tiled=True)  321 us
    all_gather x8, blocking collectives, fetch_weights(): lax.all_gather(w_qkv, 'dp', axis=0, tiled=True)  296 us
    all_gather x8, blocking collectives, fetch_weights(): lax.all_gather(w_out, 'dp', axis=1, tiled=True)  267 us
    all_gather x8, waiting for transfers between devices, fetch_weights(): lax.all_gather(w_down, 'dp', axis=1, tiled=True)  260 us
    all_gather x8, waiting for transfers between devices, fetch_weights(): lax.all_gather(w_up, 'dp', axis=0, tiled=True)  175 us
    all_gather x4, blocking collectives, fetch_weights(): lax.all_gather(biases, ('dp', 'mp'), axis=1, tiled=True)  148 us
    convert_element_type x12, other arithmetic, backward_pass(): grad_scores = (soft_weights * (grad_soft - row_delta)).astype(jnp.bfloat16)  139 us
    reduce_scatter x8, waiting for transfers between devices, project_back(): lax.psum_scatter(term(jnp.int32(0), share_rows * lax.axis_size('mp')).ast...  135 us
  transfers between devices with their start and end apart: 85, of which 52 were waited for; matrix products, arithmetic and copies ran while one was open for 8% of the time, Pallas kernels for 0%

commit v1 on v0

--- a/solution.py
+++ b/solution.py
@@ -8,6 +8,18 @@
 CLIP = 1500
 epsilon = 1e-05
 masked_score = -1e30
+
+
+def collect(x, axis, dim):
+    ways, here, step = (lax.axis_size(axis), lax.axis_index(axis), x.shape[dim])
+    line, have = (x, 1)
+    while have < ways:
+        line = jnp.concatenate(
+            [line, lax.ppermute(line, axis, [(d, (d - have) % ways) for d in range(ways)])],
+            axis=dim,
+        )
+        have = 2 * have
+    return jnp.roll(line, here * step, axis=dim)
 
 
 def passed_along(array, axis, by):
@@ -42,7 +54,7 @@
     )
     norm_rows = (
         lax.all_gather(gains, ("dp", "mp"), axis=1, tiled=True),
-        lax.all_gather(biases, ("dp", "mp"), axis=1, tiled=True),
+        collect(biases, ("dp", "mp"), 1),
     )
     return (gathered, norm_rows)
 

time: 3580 us -> 3470 us (0.969)
  blocking collectives: 1450 us -> 1300 us
    all_gather x4 -> x0, blocking collectives: 148 us -> none  [fetch_weights(): lax.all_gather(biases, ('dp', 'mp'), axis=1, tiled=True)]
  transfers between devices with their start and end apart: 85 -> 90, of which waited for: 52 -> 57; matrix products, arithmetic and copies ran while one was open for 8% -> 8% of each run, Pallas kernels for 0% -> 0%
where the time goes in v1:
time: 3470 us; the launch traced here: 3460 us
  blocking collectives  1300 us (37%)
  waiting for transfers between devices  1070 us (31%)
  matrix products  375 us (11%)
  other arithmetic  352 us (10%)
  local copies, waits for them, and re-layouts  201 us (6%)
  starting transfers between devices  130 us (4%)
    all_gather x8, blocking collectives, fetch_weights(): lax.all_gather(gains, ('dp', 'mp'), axis=1, tiled=True)  323 us
    all_gather x8, blocking collectives, fetch_weights(): lax.all_gather(w_qkv, 'dp', axis=0, tiled=True)  298 us
    all_gather x8, blocking collectives, fetch_weights(): lax.all_gather(w_out, 'dp', axis=1, tiled=True)  268 us
    all_gather x8, waiting for transfers between devices, fetch_weights(): lax.all_gather(w_down, 'dp', axis=1, tiled=True)  260 us
    all_gather x8, waiting for transfers between devices, fetch_weights(): lax.all_gather(w_up, 'dp', axis=0, tiled=True)  175 us
    convert_element_type x12, other arithmetic, backward_pass(): grad_scores = (soft_weights * (grad_soft - row_delta)).astype(jnp.bfloat16)  138 us
    reduce_scatter x8, waiting for transfers between devices, project_back(): lax.psum_scatter(term(jnp.int32(0), share_rows * lax.axis_size('mp')).ast...  135 us
    all_gather x4, blocking collectives, fetch_weights(): lax.all_gather(b_qv, 'dp', axis=2, tiled=True)  122 us
  transfers between devices with their start and end apart: 90, of which 57 were waited for; matrix products, arithmetic and copies ran while one was open for 8% of the time, Pallas kernels for 0%

profile of v1, /device:TPU:0, one launch (start us, length us, event | category | flops | bytes accessed | tf_op | source)
XLA Modules:
  0.0 3457.9 jit_solution(3565876906079245996)
XLA Ops:
  35.8 3063.9 %while.33 = (s32[]{:T(128)}, f32[768,3,192]{0,2,1:T(8,128)}, f32[2,1,192]{2,1,0:T(1,128)}, f32[192,768]{1,0:T(8,128)}, f32[768,768]{1,0:T(8,128)}, /*index=5*/f3...) while((s32[]{:T(128)}, f32[768,3,192]{0,2,1:T(8,128)}, ...), condition=%wide.region_31.32_spmd.clone.clone.clone, body=%wide.region_0.31_spmd.clone.clone.clone.sunk | while | flops 11638809600 | bytes 781708416 | solution.py:351
  40.0 45.1 %all-gather.15 = bf16[32,24,2]{1,2,0:T(2,128)(2,1)S(1)} all-gather(bf16[1,24,2]{1,2,0:T(2,128)(2,1)} %bitcast.326), channel_id=1, replica_groups=mesh['dp'=8,'mp'=4] {'dp','mp'}, dimensions={0}, use_global_device_ids=true | all-gather | bytes 3168 | tf_op jit(solution)/shard_map/while/body/eval_jaxpr/all_gather | solution.py:56
  86.0 30.5 all_gather.146
  127.4 37.6 %all_gather.144 = bf16[768,3,192]{2,1,0:T(4,128)(2,1)S(1)} all-gather(bf16[96,3,192]{2,1,0:T(4,128)(2,1)S(1)} %copy.78), channel_id=1, replica_groups=mesh['dp'=8,'mp'=4] {'dp'}, dimensions={0}, use_global_device_ids=true | all-gather | bytes 995328 | tf_op jit(solution)/shard_map/while/body/eval_jaxpr/all_gather | solution.py:48
  185.5 22.7 gather_fusion
  208.3 33.3 all_gather.147
  305.3 23.7 all-reduce.9
  361.0 34.0 all-gather.25.cloned.1.call-done
  398.4 22.3 reduce-scatter.29.cloned.1.call-done
  433.3 30.7 all-gather.27.cloned.1.call-done
  469.5 36.6 %all-gather.29.cloned.1.call-done = bf16[768,768]{1,0:T(8,128)(2,1)} async-done(((bf16[96,768]{1,0:T(8,128)(2,1)}), bf16[768,768]{1,0:T(8,128)(2,1)}) %all-gather.29.cloned.1.call-update) | async-done | bytes 1179664 | tf_op jit(solution)/shard_map/while/body/eval_jaxpr/all_gather | solution.py:51
  514.0 38.9 %all-gather.17 = bf16[32,24,2]{1,2,0:T(2,128)(2,1)S(1)} all-gather(bf16[1,24,2]{1,2,0:T(2,128)(2,1)S(1)} %bitcast.327), channel_id=1, replica_groups=mesh['dp'=8,'mp'=4] {'dp','mp'}, dimensions={0}, use_global_device_ids=true | all-gather | bytes 3168 | tf_op jit(solution)/shard_map/while/body/eval_jaxpr/all_gather | solution.py:56
  553.2 33.6 all_gather.154
  586.9 37.0 %all_gather.155 = bf16[768,3,192]{2,0,1:T(8,128)(2,1)} all-gather(bf16[96,3,192]{2,0,1:T(8,128)(2,1)S(1)} %copy-done.32), channel_id=1, replica_groups=mesh['dp'=8,'mp'=4] {'dp'}, dimensions={0}, use_global_device_ids=true | all-gather | bytes 995328 | tf_op jit(solution)/shard_map/while/body/eval_jaxpr/all_gather | solution.py:48
  762.8 35.0 %reduce-scatter.33.cloned.1.call-done = bf16[144,768]{1,0:T(8,128)(2,1)} async-done(((bf16[576,768]{1,0:T(8,128)(2,1)}), bf16[144,768]{1,0:T(8,128)(2,1)}) %reduce-scatter.33.cloned.1.call-update) | async-done | bytes 221200 | tf_op jit(solution)/shard_map/while/body/eval_jaxpr/reduce_scatter | solution.py:92
  806.9 40.7 %all-gather.15 = bf16[32,24,2]{1,2,0:T(2,128)(2,1)S(1)} all-gather(bf16[1,24,2]{1,2,0:T(2,128)(2,1)} %bitcast.326), channel_id=1, replica_groups=mesh['dp'=8,'mp'=4] {'dp','mp'}, dimensions={0}, use_global_device_ids=true | all-gather | bytes 3168 | tf_op jit(solution)/shard_map/while/body/eval_jaxpr/all_gather | solution.py:56
  848.5 30.5 all_gather.146
  890.0 37.6 %all_gather.144 = bf16[768,3,192]{2,1,0:T(4,128)(2,1)S(1)} all-gather(bf16[96,3,192]{2,1,0:T(4,128)(2,1)S(1)} %copy.78), channel_id=1, replica_groups=mesh['dp'=8,'mp'=4] {'dp'}, dimensions={0}, use_global_device_ids=true | all-gather | bytes 995328 | tf_op jit(solution)/shard_map/while/body/eval_jaxpr/all_gather | solution.py:48
  948.1 22.7 gather_fusion
  970.8 33.3 all_gather.147
  1067.9 23.6 all-reduce.9
  1123.4 34.3 all-gather.25.cloned.1.call-done
  1161.2 22.3 reduce-scatter.29.cloned.1.call-done
  1195.9 30.9 all-gather.27.cloned.1.call-done
  1232.2 36.4 %all-gather.29.cloned.1.call-done = bf16[768,768]{1,0:T(8,128)(2,1)} async-done(((bf16[96,768]{1,0:T(8,128)(2,1)}), bf16[768,768]{1,0:T(8,128)(2,1)}) %all-gather.29.cloned.1.call-update) | async-done | bytes 1179664 | tf_op jit(solution)/shard_map/while/body/eval_jaxpr/all_gather | solution.py:51
  1277.4 38.9 %all-gather.17 = bf16[32,24,2]{1,2,0:T(2,128)(2,1)S(1)} all-gather(bf16[1,24,2]{1,2,0:T(2,128)(2,1)S(1)} %bitcast.327), channel_id=1, replica_groups=mesh['dp'=8,'mp'=4] {'dp','mp'}, dimensions={0}, use_global_device_ids=true | all-gather | bytes 3168 | tf_op jit(solution)/shard_map/while/body/eval_jaxpr/all_gather | solution.py:56
  1316.6 33.6 all_gather.154
  1350.2 37.0 %all_gather.155 = bf16[768,3,192]{2,0,1:T(8,128)(2,1)} all-gather(bf16[96,3,192]{2,0,1:T(8,128)(2,1)S(1)} %copy-done.32), channel_id=1, replica_groups=mesh['dp'=8,'mp'=4] {'dp'}, dimensions={0}, use_global_device_ids=true | all-gather | bytes 995328 | tf_op jit(solution)/shard_map/while/body/eval_jaxpr/all_gather | solution.py:48
  1448.4 11.6 multiply_convert_fusion.10
  1529.6 33.2 reduce-scatter.33.cloned.1.call-done
  1572.0 40.7 %all-gather.15 = bf16[32,24,2]{1,2,0:T(2,128)(2,1)S(1)} all-gather(bf16[1,24,2]{1,2,0:T(2,128)(2,1)} %bitcast.326), channel_id=1, replica_groups=mesh['dp'=8,'mp'=4] {'dp','mp'}, dimensions={0}, use_global_device_ids=true | all-gather | bytes 3168 | tf_op jit(solution)/shard_map/while/body/eval_jaxpr/all_gather | solution.py:56
  1613.6 30.5 all_gather.146
  1655.0 37.6 %all_gather.144 = bf16[768,3,192]{2,1,0:T(4,128)(2,1)S(1)} all-gather(bf16[96,3,192]{2,1,0:T(4,128)(2,1)S(1)} %copy.78), channel_id=1, replica_groups=mesh['dp'=8,'mp'=4] {'dp'}, dimensions={0}, use_global_device_ids=true | all-gather | bytes 995328 | tf_op jit(solution)/shard_map/while/body/eval_jaxpr/all_gather | solution.py:48
  1713.1 22.7 gather_fusion
  1735.9 33.3 all_gather.147
  1832.8 23.5 all-reduce.9
  1888.3 34.1 all-gather.25.cloned.1.call-done
  1925.8 22.3 reduce-scatter.29.cloned.1.call-done
  1960.7 30.7 all-gather.27.cloned.1.call-done
  1996.8 36.6 %all-gather.29.cloned.1.call-done = bf16[768,768]{1,0:T(8,128)(2,1)} async-done(((bf16[96,768]{1,0:T(8,128)(2,1)}), bf16[768,768]{1,0:T(8,128)(2,1)}) %all-gather.29.cloned.1.call-update) | async-done | bytes 1179664 | tf_op jit(solution)/shard_map/while/body/eval_jaxpr/all_gather | solution.py:51
  2042.2 38.9 %all-gather.17 = bf16[32,24,2]{1,2,0:T(2,128)(2,1)S(1)} all-gather(bf16[1,24,2]{1,2,0:T(2,128)(2,1)S(1)} %bitcast.327), channel_id=1, replica_groups=mesh['dp'=8,'mp'=4] {'dp','mp'}, dimensions={0}, use_global_device_ids=true | all-gather | bytes 3168 | tf_op jit(solution)/shard_map/while/body/eval_jaxpr/all_gather | solution.py:56
  2081.4 33.6 all_gather.154
  2115.0 37.0 %all_gather.155 = bf16[768,3,192]{2,0,1:T(8,128)(2,1)} all-gather(bf16[96,3,192]{2,0,1:T(8,128)(2,1)S(1)} %copy-done.32), channel_id=1, replica_groups=mesh['dp'=8,'mp'=4] {'dp'}, dimensions={0}, use_global_device_ids=true | all-gather | bytes 995328 | tf_op jit(solution)/shard_map/while/body/eval_jaxpr/all_gather | solution.py:48
  2294.4 33.2 reduce-scatter.33.cloned.1.call-done
  2336.8 40.7 %all-gather.15 = bf16[32,24,2]{1,2,0:T(2,128)(2,1)S(1)} all-gather(bf16[1,24,2]{1,2,0:T(2,128)(2,1)} %bitcast.326), channel_id=1, replica_groups=mesh['dp'=8,'mp'=4] {'dp','mp'}, dimensions={0}, use_global_device_ids=true | all-gather | bytes 3168 | tf_op jit(solution)/shard_map/while/body/eval_jaxpr/all_gather | solution.py:56
  2378.4 30.5 all_gather.146
  2419.8 37.6 %all_gather.144 = bf16[768,3,192]{2,1,0:T(4,128)(2,1)S(1)} all-gather(bf16[96,3,192]{2,1,0:T(4,128)(2,1)S(1)} %copy.78), channel_id=1, replica_groups=mesh['dp'=8,'mp'=4] {'dp'}, dimensions={0}, use_global_device_ids=true | all-gather | bytes 995328 | tf_op jit(solution)/shard_map/while/body/eval_jaxpr/all_gather | solution.py:48
  2478.0 22.7 gather_fusion
  2500.7 33.3 all_gather.147
  2597.6 23.5 all-reduce.9
  2653.1 34.1 all-gather.25.cloned.1.call-done
  2690.7 22.3 reduce-scatter.29.cloned.1.call-done
  2725.5 30.7 all-gather.27.cloned.1.call-done
  2761.7 36.6 %all-gather.29.cloned.1.call-done = bf16[768,768]{1,0:T(8,128)(2,1)} async-done(((bf16[96,768]{1,0:T(8,128)(2,1)}), bf16[768,768]{1,0:T(8,128)(2,1)}) %all-gather.29.cloned.1.call-update) | async-done | bytes 1179664 | tf_op jit(solution)/shard_map/while/body/eval_jaxpr/all_gather | solution.py:51
  2807.1 38.9 %all-gather.17 = bf16[32,24,2]{1,2,0:T(2,128)(2,1)S(1)} all-gather(bf16[1,24,2]{1,2,0:T(2,128)(2,1)S(1)} %bitcast.327), channel_id=1, replica_groups=mesh['dp'=8,'mp'=4] {'dp','mp'}, dimensions={0}, use_global_device_ids=true | all-gather | bytes 3168 | tf_op jit(solution)/shard_map/while/body/eval_jaxpr/all_gather | solution.py:56
  2846.3 33.6 all_gather.154
  2879.9 37.0 %all_gather.155 = bf16[768,3,192]{2,0,1:T(8,128)(2,1)} all-gather(bf16[96,3,192]{2,0,1:T(8,128)(2,1)S(1)} %copy-done.32), channel_id=1, replica_groups=mesh['dp'=8,'mp'=4] {'dp'}, dimensions={0}, use_global_device_ids=true | all-gather | bytes 995328 | tf_op jit(solution)/shard_map/while/body/eval_jaxpr/all_gather | solution.py:48
  3059.2 33.2 reduce-scatter.33.cloned.1.call-done
  3112.3 21.4 all-reduce.4
  3133.7 37.3 %all-reduce.7 = (f32[2,768]{1,0:T(2,128)S(1)}, f32[4,768]{1,0:T(4,128)S(1)}) all-reduce(f32[2,768]{1,0:T(2,128)S(1)} %copy-done.57, f32[4,768]{1,0:T(4,128)S(1)} %copy-done.42), channel_id=13, replica_groups=mesh['dp'=8,'mp'=4] {'dp','mp'}, use_global_device_ids=true, to_apply=%region_38.39.clone | all-reduce | flops 4608 | bytes 36864
  3174.4 56.8 %reduce-scatter.23.cloned.1.call-done = f32[96,192]{1,0:T(8,128)} async-done(((f32[768,192]{1,0:T(8,128)}), f32[96,192]{1,0:T(8,128)}) %reduce-scatter.23.cloned.1.call-update) | async-done | bytes 73744
  3232.8 71.0 %reduce-scatter.17.cloned.1.call-done = f32[96,3,192]{2,0,1:T(8,128)} async-done(((f32[768,3,192]{2,0,1:T(8,128)}), f32[96,3,192]{2,0,1:T(8,128)}) %reduce-scatter.17.cloned.1.call-update) | async-done | bytes 221200 | tf_op jit(solution)/shard_map/reduce_scatter | solution.py:353
  3303.9 73.0 %reduce-scatter.19.cloned.1.call-done = f32[96,768]{1,0:T(8,128)} async-done(((f32[768,768]{1,0:T(8,128)}), f32[96,768]{1,0:T(8,128)}) %reduce-scatter.19.cloned.1.call-update) | async-done | bytes 294928 | tf_op jit(solution)/shard_map/reduce_scatter | solution.py:356
  3376.8 73.0 %reduce-scatter.21.cloned.1.call-done = f32[768,96]{0,1:T(8,128)} async-done(((f32[768,768]{0,1:T(8,128)}), f32[768,96]{0,1:T(8,128)}) %reduce-scatter.21.cloned.1.call-update) | async-done | bytes 294928 | tf_op jit(solution)/shard_map/reduce_scatter | solution.py:358
  (1381 shorter events, 1258.8 us)
Async XLA Ops:
  35.8 297.4 %reduce-scatter.27.cloned.1.call-start = ((), (), s32[]{:S(2)}) async-start(), calls=%async_computation.14 | async-start | bytes 1105920 | tf_op jit(solution)/shard_map/while/body/eval_jaxpr/reduce_scatter | solution.py:76
  167.0 74.6 %collective-permute-start.5 = (bf16[576,2,192]{0,2,1:T(8,128)(2,1)S(1)}, bf16[576,2,192]{0,2,1:T(8,128)(2,1)S(1)}, u32[]{:S(2)}, u32[]{:S(2)}) collective-permute-start(bf16[576,2,192]{0,2,1:T(8,128)(2,1)S(1)} %slice.568), channel_id=1, source_target_pairs={{12,0},{16,4},{20,8},{24,12},{28,16},{13,1},{17,5},{21,9},{25,13},... | collective-permute-start | bytes 1327112 | tf_op jit(solution)/shard_map/while/body/eval_jaxpr/ppermute | solution.py:28
  168.3 77.0 %collective-permute-start.4 = (bf16[576,2,192]{0,2,1:T(8,128)(2,1)S(1)}, bf16[576,2,192]{0,2,1:T(8,128)(2,1)S(1)}, u32[]{:S(2)}, u32[]{:S(2)}) collective-permute-start(bf16[576,2,192]{0,2,1:T(8,128)(2,1)S(1)} %slice.568), channel_id=1, source_target_pairs={{8,0},{12,4},{16,8},{20,12},{24,16},{28,20},{9,1},{13,5},{17,9},{2... | collective-permute-start | bytes 1327112 | tf_op jit(solution)/shard_map/while/body/eval_jaxpr/ppermute | solution.py:28
  169.6 75.8 %collective-permute-start.3 = (bf16[576,2,192]{0,2,1:T(8,128)(2,1)S(1)}, bf16[576,2,192]{0,2,1:T(8,128)(2,1)S(1)}, u32[]{:S(2)}, u32[]{:S(2)}) collective-permute-start(bf16[576,2,192]{0,2,1:T(8,128)(2,1)S(1)} %slice.568), channel_id=1, source_target_pairs={{4,0},{8,4},{12,8},{16,12},{20,16},{24,20},{28,24},{5,1},{9,5},{13... | collective-permute-start | bytes 1327112 | tf_op jit(solution)/shard_map/while/body/eval_jaxpr/ppermute | solution.py:28
  170.9 74.5 %collective-permute-start.2 = (bf16[576,2,192]{0,2,1:T(8,128)(2,1)S(1)}, bf16[576,2,192]{0,2,1:T(8,128)(2,1)}, u32[]{:S(2)}, u32[]{:S(2)}) collective-permute-start(bf16[576,2,192]{0,2,1:T(8,128)(2,1)S(1)} %slice.568), channel_id=1, source_target_pairs={{0,4},{4,8},{8,12},{12,16},{16,20},{20,24},{24,28},{1,5},{5,9},{9,... | collective-permute-start | bytes 1327112 | tf_op jit(solution)/shard_map/while/body/eval_jaxpr/ppermute | solution.py:28
  176.3 69.1 %collective-permute-start.1 = (bf16[576,2,192]{0,2,1:T(8,128)(2,1)S(1)}, bf16[576,2,192]{0,2,1:T(8,128)(2,1)}, u32[]{:S(2)}, u32[]{:S(2)}) collective-permute-start(bf16[576,2,192]{0,2,1:T(8,128)(2,1)S(1)} %slice.568), channel_id=1, source_target_pairs={{0,8},{4,12},{8,16},{12,20},{16,24},{20,28},{1,9},{5,13},{9,17},{1... | collective-permute-start | bytes 1327112 | tf_op jit(solution)/shard_map/while/body/eval_jaxpr/ppermute | solution.py:28
  302.6 50.5 %all-gather.23.cloned.1.call-start = ((), (), s32[]{:S(2)}) async-start(), calls=%async_computation.15 | async-start | bytes 1327104 | tf_op jit(solution)/shard_map/while/body/eval_jaxpr/all_gather | solution.py:51
  303.2 91.8 %all-gather.25.cloned.1.call-start = ((), (), s32[]{:S(2)}) async-start(), calls=%async_computation.16 | async-start | bytes 1327104 | tf_op jit(solution)/shard_map/while/body/eval_jaxpr/all_gather | solution.py:53
  303.8 117.0 %reduce-scatter.29.cloned.1.call-start = ((), (), s32[]{:S(2)}) async-start(), calls=%async_computation.17 | async-start | bytes 1105920 | tf_op jit(solution)/shard_map/while/body/eval_jaxpr/reduce_scatter | solution.py:76
  398.4 65.6 %all-gather.27.cloned.1.call-start = ((), (), s32[]{:S(2)}) async-start(), calls=%async_computation.18 | async-start | bytes 1327104 | tf_op jit(solution)/shard_map/while/body/eval_jaxpr/all_gather | solution.py:53
  422.5 83.5 %all-gather.29.cloned.1.call-start = ((), (), s32[]{:S(2)}) async-start(), calls=%async_computation.19 | async-start | bytes 1327104 | tf_op jit(solution)/shard_map/while/body/eval_jaxpr/all_gather | solution.py:51
  423.2 203.2 %reduce-scatter.31.cloned.1.call-start = ((), (), s32[]{:S(2)}) async-start(), calls=%async_computation.20 | async-start | bytes 1105920 | tf_op jit(solution)/shard_map/while/body/eval_jaxpr/reduce_scatter | solution.py:92
  509.4 288.4 %reduce-scatter.33.cloned.1.call-start = ((), (), s32[]{:S(2)}) async-start(), calls=%async_computation.21 | async-start | bytes 1105920 | tf_op jit(solution)/shard_map/while/body/eval_jaxpr/reduce_scatter | solution.py:92
  719.9 26.7 collective-permute-start.8
  729.8 24.0 collective-permute-start.11
  802.7 292.6 %reduce-scatter.27.cloned.1.call-start = ((), (), s32[]{:S(2)}) async-start(), calls=%async_computation.14 | async-start | bytes 1105920 | tf_op jit(solution)/shard_map/while/body/eval_jaxpr/reduce_scatter | solution.py:76
  929.5 74.6 %collective-permute-start.5 = (bf16[576,2,192]{0,2,1:T(8,128)(2,1)S(1)}, bf16[576,2,192]{0,2,1:T(8,128)(2,1)S(1)}, u32[]{:S(2)}, u32[]{:S(2)}) collective-permute-start(bf16[576,2,192]{0,2,1:T(8,128)(2,1)S(1)} %slice.568), channel_id=1, source_target_pairs={{12,0},{16,4},{20,8},{24,12},{28,16},{13,1},{17,5},{21,9},{25,13},... | collective-permute-start | bytes 1327112 | tf_op jit(solution)/shard_map/while/body/eval_jaxpr/ppermute | solution.py:28
  930.8 77.1 %collective-permute-start.4 = (bf16[576,2,192]{0,2,1:T(8,128)(2,1)S(1)}, bf16[576,2,192]{0,2,1:T(8,128)(2,1)S(1)}, u32[]{:S(2)}, u32[]{:S(2)}) collective-permute-start(bf16[576,2,192]{0,2,1:T(8,128)(2,1)S(1)} %slice.568), channel_id=1, source_target_pairs={{8,0},{12,4},{16,8},{20,12},{24,16},{28,20},{9,1},{13,5},{17,9},{2... | collective-permute-start | bytes 1327112 | tf_op jit(solution)/shard_map/while/body/eval_jaxpr/ppermute | solution.py:28
  932.1 75.9 %collective-permute-start.3 = (bf16[576,2,192]{0,2,1:T(8,128)(2,1)S(1)}, bf16[576,2,192]{0,2,1:T(8,128)(2,1)S(1)}, u32[]{:S(2)}, u32[]{:S(2)}) collective-permute-start(bf16[576,2,192]{0,2,1:T(8,128)(2,1)S(1)} %slice.568), channel_id=1, source_target_pairs={{4,0},{8,4},{12,8},{16,12},{20,16},{24,20},{28,24},{5,1},{9,5},{13... | collective-permute-start | bytes 1327112 | tf_op jit(solution)/shard_map/while/body/eval_jaxpr/ppermute | solution.py:28
  933.4 74.6 %collective-permute-start.2 = (bf16[576,2,192]{0,2,1:T(8,128)(2,1)S(1)}, bf16[576,2,192]{0,2,1:T(8,128)(2,1)}, u32[]{:S(2)}, u32[]{:S(2)}) collective-permute-start(bf16[576,2,192]{0,2,1:T(8,128)(2,1)S(1)} %slice.568), channel_id=1, source_target_pairs={{0,4},{4,8},{8,12},{12,16},{16,20},{20,24},{24,28},{1,5},{5,9},{9,... | collective-permute-start | bytes 1327112 | tf_op jit(solution)/shard_map/while/body/eval_jaxpr/ppermute | solution.py:28
  938.8 69.2 %collective-permute-start.1 = (bf16[576,2,192]{0,2,1:T(8,128)(2,1)S(1)}, bf16[576,2,192]{0,2,1:T(8,128)(2,1)}, u32[]{:S(2)}, u32[]{:S(2)}) collective-permute-start(bf16[576,2,192]{0,2,1:T(8,128)(2,1)S(1)} %slice.568), channel_id=1, source_target_pairs={{0,8},{4,12},{8,16},{12,20},{16,24},{20,28},{1,9},{5,13},{9,17},{1... | collective-permute-start | bytes 1327112 | tf_op jit(solution)/shard_map/while/body/eval_jaxpr/ppermute | solution.py:28
  1064.8 50.7 %all-gather.23.cloned.1.call-start = ((), (), s32[]{:S(2)}) async-start(), calls=%async_computation.15 | async-start | bytes 1327104 | tf_op jit(solution)/shard_map/while/body/eval_jaxpr/all_gather | solution.py:51
  1065.6 92.1 %all-gather.25.cloned.1.call-start = ((), (), s32[]{:S(2)}) async-start(), calls=%async_computation.16 | async-start | bytes 1327104 | tf_op jit(solution)/shard_map/while/body/eval_jaxpr/all_gather | solution.py:53
  1066.3 117.1 %reduce-scatter.29.cloned.1.call-start = ((), (), s32[]{:S(2)}) async-start(), calls=%async_computation.17 | async-start | bytes 1105920 | tf_op jit(solution)/shard_map/while/body/eval_jaxpr/reduce_scatter | solution.py:76
  1161.1 65.6 %all-gather.27.cloned.1.call-start = ((), (), s32[]{:S(2)}) async-start(), calls=%async_computation.18 | async-start | bytes 1327104 | tf_op jit(solution)/shard_map/while/body/eval_jaxpr/all_gather | solution.py:53
  1185.2 83.4 %all-gather.29.cloned.1.call-start = ((), (), s32[]{:S(2)}) async-start(), calls=%async_computation.19 | async-start | bytes 1327104 | tf_op jit(solution)/shard_map/while/body/eval_jaxpr/all_gather | solution.py:51
  1185.8 205.7 %reduce-scatter.31.cloned.1.call-start = ((), (), s32[]{:S(2)}) async-start(), calls=%async_computation.20 | async-start | bytes 1105920 | tf_op jit(solution)/shard_map/while/body/eval_jaxpr/reduce_scatter | solution.py:92
  1272.0 290.8 %reduce-scatter.33.cloned.1.call-start = ((), (), s32[]{:S(2)}) async-start(), calls=%async_computation.21 | async-start | bytes 1105920 | tf_op jit(solution)/shard_map/while/body/eval_jaxpr/reduce_scatter | solution.py:92
  1485.0 26.7 collective-permute-start.8
  1494.9 24.0 collective-permute-start.11
  1567.7 292.6 %reduce-scatter.27.cloned.1.call-start = ((), (), s32[]{:S(2)}) async-start(), calls=%async_computation.14 | async-start | bytes 1105920 | tf_op jit(solution)/shard_map/while/body/eval_jaxpr/reduce_scatter | solution.py:76
  1694.6 74.6 %collective-permute-start.5 = (bf16[576,2,192]{0,2,1:T(8,128)(2,1)S(1)}, bf16[576,2,192]{0,2,1:T(8,128)(2,1)S(1)}, u32[]{:S(2)}, u32[]{:S(2)}) collective-permute-start(bf16[576,2,192]{0,2,1:T(8,128)(2,1)S(1)} %slice.568), channel_id=1, source_target_pairs={{12,0},{16,4},{20,8},{24,12},{28,16},{13,1},{17,5},{21,9},{25,13},... | collective-permute-start | bytes 1327112 | tf_op jit(solution)/shard_map/while/body/eval_jaxpr/ppermute | solution.py:28
  1695.9 77.1 %collective-permute-start.4 = (bf16[576,2,192]{0,2,1:T(8,128)(2,1)S(1)}, bf16[576,2,192]{0,2,1:T(8,128)(2,1)S(1)}, u32[]{:S(2)}, u32[]{:S(2)}) collective-permute-start(bf16[576,2,192]{0,2,1:T(8,128)(2,1)S(1)} %slice.568), channel_id=1, source_target_pairs={{8,0},{12,4},{16,8},{20,12},{24,16},{28,20},{9,1},{13,5},{17,9},{2... | collective-permute-start | bytes 1327112 | tf_op jit(solution)/shard_map/while/body/eval_jaxpr/ppermute | solution.py:28
  1697.2 75.9 %collective-permute-start.3 = (bf16[576,2,192]{0,2,1:T(8,128)(2,1)S(1)}, bf16[576,2,192]{0,2,1:T(8,128)(2,1)S(1)}, u32[]{:S(2)}, u32[]{:S(2)}) collective-permute-start(bf16[576,2,192]{0,2,1:T(8,128)(2,1)S(1)} %slice.568), channel_id=1, source_target_pairs={{4,0},{8,4},{12,8},{16,12},{20,16},{24,20},{28,24},{5,1},{9,5},{13... | collective-permute-start | bytes 1327112 | tf_op jit(solution)/shard_map/while/body/eval_jaxpr/ppermute | solution.py:28
  1698.5 74.6 %collective-permute-start.2 = (bf16[576,2,192]{0,2,1:T(8,128)(2,1)S(1)}, bf16[576,2,192]{0,2,1:T(8,128)(2,1)}, u32[]{:S(2)}, u32[]{:S(2)}) collective-permute-start(bf16[576,2,192]{0,2,1:T(8,128)(2,1)S(1)} %slice.568), channel_id=1, source_target_pairs={{0,4},{4,8},{8,12},{12,16},{16,20},{20,24},{24,28},{1,5},{5,9},{9,... | collective-permute-start | bytes 1327112 | tf_op jit(solution)/shard_map/while/body/eval_jaxpr/ppermute | solution.py:28
  1703.9 69.2 %collective-permute-start.1 = (bf16[576,2,192]{0,2,1:T(8,128)(2,1)S(1)}, bf16[576,2,192]{0,2,1:T(8,128)(2,1)}, u32[]{:S(2)}, u32[]{:S(2)}) collective-permute-start(bf16[576,2,192]{0,2,1:T(8,128)(2,1)S(1)} %slice.568), channel_id=1, source_target_pairs={{0,8},{4,12},{8,16},{12,20},{16,24},{20,28},{1,9},{5,13},{9,17},{1... | collective-permute-start | bytes 1327112 | tf_op jit(solution)/shard_map/while/body/eval_jaxpr/ppermute | solution.py:28
  1829.9 50.5 %all-gather.23.cloned.1.call-start = ((), (), s32[]{:S(2)}) async-start(), calls=%async_computation.15 | async-start | bytes 1327104 | tf_op jit(solution)/shard_map/while/body/eval_jaxpr/all_gather | solution.py:51
  1830.4 91.9 %all-gather.25.cloned.1.call-start = ((), (), s32[]{:S(2)}) async-start(), calls=%async_computation.16 | async-start | bytes 1327104 | tf_op jit(solution)/shard_map/while/body/eval_jaxpr/all_gather | solution.py:53
  1831.2 116.9 %reduce-scatter.29.cloned.1.call-start = ((), (), s32[]{:S(2)}) async-start(), calls=%async_computation.17 | async-start | bytes 1105920 | tf_op jit(solution)/shard_map/while/body/eval_jaxpr/reduce_scatter | solution.py:76
  1925.8 65.6 %all-gather.27.cloned.1.call-start = ((), (), s32[]{:S(2)}) async-start(), calls=%async_computation.18 | async-start | bytes 1327104 | tf_op jit(solution)/shard_map/while/body/eval_jaxpr/all_gather | solution.py:53
  1949.9 83.5 %all-gather.29.cloned.1.call-start = ((), (), s32[]{:S(2)}) async-start(), calls=%async_computation.19 | async-start | bytes 1327104 | tf_op jit(solution)/shard_map/while/body/eval_jaxpr/all_gather | solution.py:51
  1950.6 205.7 %reduce-scatter.31.cloned.1.call-start = ((), (), s32[]{:S(2)}) async-start(), calls=%async_computation.20 | async-start | bytes 1105920 | tf_op jit(solution)/shard_map/while/body/eval_jaxpr/reduce_scatter | solution.py:92
  2036.8 290.8 %reduce-scatter.33.cloned.1.call-start = ((), (), s32[]{:S(2)}) async-start(), calls=%async_computation.21 | async-start | bytes 1105920 | tf_op jit(solution)/shard_map/while/body/eval_jaxpr/reduce_scatter | solution.py:92
  2249.8 26.7 collective-permute-start.8
  2259.7 24.0 collective-permute-start.11
  2332.6 292.6 %reduce-scatter.27.cloned.1.call-start = ((), (), s32[]{:S(2)}) async-start(), calls=%async_computation.14 | async-start | bytes 1105920 | tf_op jit(solution)/shard_map/while/body/eval_jaxpr/reduce_scatter | solution.py:76
  2459.4 74.6 %collective-permute-start.5 = (bf16[576,2,192]{0,2,1:T(8,128)(2,1)S(1)}, bf16[576,2,192]{0,2,1:T(8,128)(2,1)S(1)}, u32[]{:S(2)}, u32[]{:S(2)}) collective-permute-start(bf16[576,2,192]{0,2,1:T(8,128)(2,1)S(1)} %slice.568), channel_id=1, source_target_pairs={{12,0},{16,4},{20,8},{24,12},{28,16},{13,1},{17,5},{21,9},{25,13},... | collective-permute-start | bytes 1327112 | tf_op jit(solution)/shard_map/while/body/eval_jaxpr/ppermute | solution.py:28
  2460.7 77.1 %collective-permute-start.4 = (bf16[576,2,192]{0,2,1:T(8,128)(2,1)S(1)}, bf16[576,2,192]{0,2,1:T(8,128)(2,1)S(1)}, u32[]{:S(2)}, u32[]{:S(2)}) collective-permute-start(bf16[576,2,192]{0,2,1:T(8,128)(2,1)S(1)} %slice.568), channel_id=1, source_target_pairs={{8,0},{12,4},{16,8},{20,12},{24,16},{28,20},{9,1},{13,5},{17,9},{2... | collective-permute-start | bytes 1327112 | tf_op jit(solution)/shard_map/while/body/eval_jaxpr/ppermute | solution.py:28
  2462.0 75.9 %collective-permute-start.3 = (bf16[576,2,192]{0,2,1:T(8,128)(2,1)S(1)}, bf16[576,2,192]{0,2,1:T(8,128)(2,1)S(1)}, u32[]{:S(2)}, u32[]{:S(2)}) collective-permute-start(bf16[576,2,192]{0,2,1:T(8,128)(2,1)S(1)} %slice.568), channel_id=1, source_target_pairs={{4,0},{8,4},{12,8},{16,12},{20,16},{24,20},{28,24},{5,1},{9,5},{13... | collective-permute-start | bytes 1327112 | tf_op jit(solution)/shard_map/while/body/eval_jaxpr/ppermute | solution.py:28
  2463.3 74.6 %collective-permute-start.2 = (bf16[576,2,192]{0,2,1:T(8,128)(2,1)S(1)}, bf16[576,2,192]{0,2,1:T(8,128)(2,1)}, u32[]{:S(2)}, u32[]{:S(2)}) collective-permute-start(bf16[576,2,192]{0,2,1:T(8,128)(2,1)S(1)} %slice.568), channel_id=1, source_target_pairs={{0,4},{4,8},{8,12},{12,16},{16,20},{20,24},{24,28},{1,5},{5,9},{9,... | collective-permute-start | bytes 1327112 | tf_op jit(solution)/shard_map/while/body/eval_jaxpr/ppermute | solution.py:28
  2468.7 69.2 %collective-permute-start.1 = (bf16[576,2,192]{0,2,1:T(8,128)(2,1)S(1)}, bf16[576,2,192]{0,2,1:T(8,128)(2,1)}, u32[]{:S(2)}, u32[]{:S(2)}) collective-permute-start(bf16[576,2,192]{0,2,1:T(8,128)(2,1)S(1)} %slice.568), channel_id=1, source_target_pairs={{0,8},{4,12},{8,16},{12,20},{16,24},{20,28},{1,9},{5,13},{9,17},{1... | collective-permute-start | bytes 1327112 | tf_op jit(solution)/shard_map/while/body/eval_jaxpr/ppermute | solution.py:28
  2594.7 50.5 %all-gather.23.cloned.1.call-start = ((), (), s32[]{:S(2)}) async-start(), calls=%async_computation.15 | async-start | bytes 1327104 | tf_op jit(solution)/shard_map/while/body/eval_jaxpr/all_gather | solution.py:51
  2595.3 91.9 %all-gather.25.cloned.1.call-start = ((), (), s32[]{:S(2)}) async-start(), calls=%async_computation.16 | async-start | bytes 1327104 | tf_op jit(solution)/shard_map/while/body/eval_jaxpr/all_gather | solution.py:53
  2596.0 117.0 %reduce-scatter.29.cloned.1.call-start = ((), (), s32[]{:S(2)}) async-start(), calls=%async_computation.17 | async-start | bytes 1105920 | tf_op jit(solution)/shard_map/while/body/eval_jaxpr/reduce_scatter | solution.py:76
  2690.6 65.6 %all-gather.27.cloned.1.call-start = ((), (), s32[]{:S(2)}) async-start(), calls=%async_computation.18 | async-start | bytes 1327104 | tf_op jit(solution)/shard_map/while/body/eval_jaxpr/all_gather | solution.py:53
  2714.7 83.5 %all-gather.29.cloned.1.call-start = ((), (), s32[]{:S(2)}) async-start(), calls=%async_computation.19 | async-start | bytes 1327104 | tf_op jit(solution)/shard_map/while/body/eval_jaxpr/all_gather | solution.py:51
  2715.5 205.7 %reduce-scatter.31.cloned.1.call-start = ((), (), s32[]{:S(2)}) async-start(), calls=%async_computation.20 | async-start | bytes 1105920 | tf_op jit(solution)/shard_map/while/body/eval_jaxpr/reduce_scatter | solution.py:92
  2801.6 290.8 %reduce-scatter.33.cloned.1.call-start = ((), (), s32[]{:S(2)}) async-start(), calls=%async_computation.21 | async-start | bytes 1105920 | tf_op jit(solution)/shard_map/while/body/eval_jaxpr/reduce_scatter | solution.py:92
  3014.7 26.7 collective-permute-start.8
  3099.7 73.3 %reduce-scatter.25.cloned.1.call-start = ((), (), s32[]{:S(2)}) async-start(), calls=%async_computation.13 | async-start | bytes 442368
  3101.4 129.8 %reduce-scatter.23.cloned.1.call-start = ((), (), s32[]{:S(2)}) async-start(), calls=%async_computation.12 | async-start | bytes 884736
  3103.7 200.1 %reduce-scatter.17.cloned.1.call-start = ((), (), s32[]{:S(2)}) async-start(), calls=%async_computation.9 | async-start | bytes 2654208 | tf_op jit(solution)/shard_map/reduce_scatter | solution.py:353
  3106.8 270.1 %reduce-scatter.19.cloned.1.call-start = ((), (), s32[]{:S(2)}) async-start(), calls=%async_computation.10 | async-start | bytes 2654208 | tf_op jit(solution)/shard_map/reduce_scatter | solution.py:356
  3107.4 342.5 %reduce-scatter.21.cloned.1.call-start = ((), (), s32[]{:S(2)}) async-start(), calls=%async_computation.11 | async-start | bytes 2654208 | tf_op jit(solution)/shard_map/reduce_scatter | solution.py:358
  (347 other events, 7189.9 us)
Sparse Core Ops, SparseCore 0:
  302.7 30.4 reduce-scatter.26
  398.5 22.1 reduce-scatter.28
  509.5 22.1 reduce-scatter.30
  756.6 41.1 reduce-scatter.32
  1064.9 30.3 reduce-scatter.26
  1161.2 22.1 reduce-scatter.28
  1272.1 22.1 reduce-scatter.30
  1521.6 41.1 reduce-scatter.32
  1830.0 30.3 reduce-scatter.26
  1925.9 22.1 reduce-scatter.28
  2036.9 22.1 reduce-scatter.30
  2286.4 41.1 reduce-scatter.32
  2594.8 30.3 reduce-scatter.26
  2690.8 22.1 reduce-scatter.28
  2801.8 22.1 reduce-scatter.30
  3051.3 41.1 reduce-scatter.32
  3103.5 62.2 reduce-scatter.24
  3168.9 62.2 reduce-scatter.22
  3235.3 68.5 reduce-scatter.16
  3307.8 69.0 reduce-scatter.18
  3380.9 68.8 reduce-scatter.20
Sparse Core Ops, SparseCore 1:
  305.3 47.8 all-gather.22
  355.2 39.7 all-gather.24
  422.6 41.4 all-gather.26
  466.2 39.7 all-gather.28
  1067.8 47.7 all-gather.22
  1117.7 39.9 all-gather.24
  1185.3 41.4 all-gather.26
  1228.8 39.7 all-gather.28
  1832.5 47.8 all-gather.22
  1882.6 39.7 all-gather.24
  1950.0 41.4 all-gather.26
  1993.6 39.7 all-gather.28
  2597.4 47.8 all-gather.22
  2647.4 39.7 all-gather.24
  2714.8 41.4 all-gather.26
  2758.5 39.7 all-gather.28
